TPU v7x, 32 devices: a whole 2x2x4 slice. The times are simulated.
32 devices in a mesh: ia: 2 (over y), ja: 4 (over x, core), ka: 4 (over z).
Axes of the slice: x: 2, y: 2, z: 4, core: 2. Of those that a mesh axis runs over, the one named last changes fastest.
Arguments:
- tensor: float32 [32, 256, 8192], P('ia', 'ka', 'ja'), may hold values from -6 to 6
- factor_b: float32 [8192, 64], P(('ja', 'ka')), may hold values from -1 to 1
- factor_c: float32 [256, 64], P('ka'), may hold values from -1 to 1
Outputs:
- factor_a: float32 [32, 64], P(('ia', 'ja', 'ka'))
- mode_two: float32 [64, 4, 2048], P(None, 'ja', ('ia', 'ka'))
All inputs are finite; a program needn't handle non-finite values.
Results may differ from a plain program's by a relative error of at most 0.00026.
Values sent between devices are 32-bit elements; how exact they have to be, the bound alone decides.
No kernel may reach another device: no remote copies, remote signals or barrier semaphores. Data moves between devices by JAX's collectives and lax.ppermute only.
A program may use at most 64 MiB of HBM per device.

v0:
```python
import functools

import jax
import jax.numpy as jnp
from jax import lax
from jax.experimental import pallas as pl
from jax.experimental.pallas import tpu as pltpu
from jax.sharding import PartitionSpec as P


F32 = jnp.float32
BF16 = jnp.bfloat16
HIGHEST = lax.Precision.HIGHEST
LANES = 128
SUBLANES = 8
VMEM = pl.BlockSpec(memory_space=pltpu.VMEM)
HBM = pl.BlockSpec(memory_space=pltpu.HBM)
NN = (((1,), (0,)), ((), ()))
NT = (((1,), (1,)), ((), ()))
TN = (((0,), (0,)), ((), ()))


def dot(a, b, dims):
    return lax.dot_general(a, b, dims, precision=HIGHEST, preferred_element_type=F32)


def cost(flops, bytes_accessed):
    return pl.CostEstimate(flops=flops, bytes_accessed=bytes_accessed, transcendentals=0)


def placed_in(x, space):
    return pltpu.with_memory_space_constraint(x, space)


def fold(square):
    half = square.shape[0] // 2
    return jnp.concatenate([square[:half, :], square[half:, :]], axis=1)


def unfold(folded):
    half = folded.shape[1] // 2
    return jnp.concatenate([folded[:, :half], folded[:, half:]], axis=0)


def total_of(refs, start=0, stop=None):
    total = refs[0][start:stop, :]
    for ref in refs[1:]:
        total = total + ref[start:stop, :]
    return total


def contract_kernel(
    x_hbm, c_hbm, q_ref, gram_ref, x_ref, c_ref, lhs_ref, x_sems, c_sem, *, chunks
):
    rows = q_ref.shape[0] // chunks
    copies = [
        pltpu.make_async_copy(
            x_hbm.at[pl.ds(n * rows, rows)], x_ref.at[pl.ds(n * rows, rows)], x_sems.at[n]
        )
        for n in range(chunks)
    ]
    c_copy = pltpu.make_async_copy(c_hbm, c_ref, c_sem)
    c_copy.start()
    for copy in copies:
        copy.start()
    c_copy.wait()
    c = c_ref[...]
    gram_ref[...] = fold(dot(c, c, TN))
    ct = c.T
    high = ct.astype(BF16)
    low = (ct - high.astype(F32)).astype(BF16)
    lhs_ref[...] = jnp.concatenate([high, low, high, low], axis=1)
    for n, copy in enumerate(copies):
        copy.wait()
        for i in range(n * rows, (n + 1) * rows):
            x = x_ref[i]
            high = x.astype(BF16)
            low = (x - high.astype(F32)).astype(BF16)
            rhs = jnp.concatenate([high, high, low, low], axis=0)
            q_ref[i] = jnp.dot(lhs_ref[...], rhs, preferred_element_type=F32)


def contract(tensor, factor_c):
    row_block, depth, width = tensor.shape
    rank = factor_c.shape[1]
    chunks = 4
    return pl.pallas_call(
        functools.partial(contract_kernel, chunks=chunks),
        out_shape=(
            pltpu.VMEM((row_block, rank, width), F32),
            pltpu.VMEM((rank // 2, 2 * rank), F32),
        ),
        in_specs=[HBM, HBM],
        out_specs=[VMEM, VMEM],
        scratch_shapes=[
            pltpu.VMEM(tensor.shape, F32),
            pltpu.VMEM(factor_c.shape, F32),
            pltpu.VMEM((rank, 4 * depth), BF16),
            pltpu.SemaphoreType.DMA((chunks,)),
            pltpu.SemaphoreType.DMA,
        ],
        compiler_params=pltpu.CompilerParams(vmem_limit_bytes=12 << 20),
        cost_estimate=cost(8 * row_block * depth * rank * width, 4 * row_block * depth * width),
        name="contract",
    )(placed_in(tensor, pltpu.HBM), placed_in(factor_c, pltpu.HBM))


def gram_terms(part_refs, rank):
    stacks = []
    for part in part_refs:
        value = part[:rank, :]
        first = value.astype(BF16)
        value = value - first.astype(F32)
        second = value.astype(BF16)
        third = (value - second.astype(F32)).astype(BF16)
        stacks.append(jnp.concatenate([first, second, third], axis=0))
    stack = jnp.concatenate(stacks, axis=1)
    terms = lax.dot_general(stack, stack, NT, preferred_element_type=F32)
    terms = terms[:, 2 * rank :] + terms[:, rank : 2 * rank] + terms[:, :rank]
    return terms[2 * rank :, :] + terms[rank : 2 * rank, :] + terms[:rank, :]


def weighted_sums(q_ref, part_refs, shifts):
    row_block, rank, _ = q_ref.shape
    width = part_refs[0].shape[1]
    here = lax.axis_index("ka")
    for tile in range(rank // SUBLANES):
        rows = pl.ds(tile * SUBLANES, SUBLANES)
        for i in range(row_block):
            total = None
            for s, part in zip(shifts, part_refs):
                start = (here ^ s) * width
                for c in range(0, width, LANES):
                    columns = pl.ds(pl.multiple_of(start + c, LANES), LANES)
                    term = q_ref[i, rows, columns] * part[rows, c : c + LANES]
                    total = term if total is None else total + term
            yield tile, i, total


def early_kernel(q_ref, *refs, shifts):
    part_refs, (sums_ref, gram_ref) = refs[:-2], refs[-2:]
    row_block, rank, _ = q_ref.shape
    gram_ref[...] = fold(gram_terms(part_refs, rank))
    for tile, i, total in weighted_sums(q_ref, part_refs, shifts):
        at = (tile * row_block + i) * SUBLANES
        sums_ref[at : at + SUBLANES, :] = total


def late_kernel(q_ref, sums_ref, gram_ref, *refs, shifts):
    part_refs, out_ref = refs[:-1], refs[-1]
    row_block, rank, _ = q_ref.shape
    half = rank // 2
    gram = fold(gram_terms(part_refs, rank))
    lane = lax.broadcasted_iota(jnp.int32, (SUBLANES, LANES), 1)
    groups = (out_ref.shape[0] - half) // SUBLANES
    packed = [jnp.zeros((SUBLANES, LANES), F32) for _ in range(groups)]
    for tile, i, total in weighted_sums(q_ref, part_refs, shifts):
        at = (tile * row_block + i) * SUBLANES
        total = total + sums_ref[at : at + SUBLANES, :]
        group, place = divmod(tile * row_block + i, LANES)
        packed[group] = jnp.where(
            lane == place, jnp.sum(total, axis=1, keepdims=True), packed[group]
        )
    for group, value in enumerate(packed):
        start = half + group * SUBLANES
        out_ref[start : start + SUBLANES, :] = value
    out_ref[:half, :] = gram + gram_ref[...]


def mode_one_sums(q, parts):
    row_block, rank, width = q.shape
    lines = row_block * rank // LANES
    count = len(parts)
    split = {0, count - 1}
    early = [s for s in range(count) if s in split]
    late = [s for s in reversed(range(count)) if s not in split]
    params = pltpu.CompilerParams(vmem_limit_bytes=6 << 20)
    work = cost(row_block * rank * width, 2 * row_block * rank * width)
    q = placed_in(q, pltpu.VMEM)
    sums, gram = pl.pallas_call(
        functools.partial(early_kernel, shifts=early),
        out_shape=(
            pltpu.VMEM((row_block * rank, LANES), F32),
            pltpu.VMEM((rank // 2, 2 * rank), F32),
        ),
        in_specs=[VMEM] * (1 + len(early)),
        out_specs=[VMEM] * 2,
        compiler_params=params,
        cost_estimate=work,
        name="mode_one_early",
    )(q, *[parts[s] for s in early])
    return pl.pallas_call(
        functools.partial(late_kernel, shifts=late),
        out_shape=pltpu.VMEM((rank // 2 + lines, LANES), F32),
        in_specs=[VMEM] * (3 + len(late)),
        out_specs=VMEM,
        compiler_params=params,
        cost_estimate=work,
        name="mode_one_late",
    )(q, sums, gram, *[parts[s] for s in late])


def add_kernel(*refs):
    part_refs, out_ref = refs[:-1], refs[-1]
    out_ref[...] = total_of(part_refs, part_refs[0].shape[0] - out_ref.shape[0])


def add_tail(parts, lines):
    return pl.pallas_call(
        add_kernel,
        out_shape=pltpu.VMEM((lines, LANES), F32),
        in_specs=[VMEM] * len(parts),
        out_specs=VMEM,
        compiler_params=pltpu.CompilerParams(vmem_limit_bytes=2 << 20),
        name="add_tail",
    )(*parts)


def solve_rows(pivot, rows):
    count = len(rows)
    rows = list(rows)
    block = {(q, s): pivot[q][s] for q in range(count) for s in range(q, count)}
    upper = {}
    for m in range(0, count, 2):
        a, b, d = block[m, m], block[m, m + 1], block[m + 1, m + 1]
        scale = 1.0 / (a * d - b * b)
        a, b, d = a * scale, b * scale, d * scale
        rows[m], rows[m + 1] = d * rows[m] - b * rows[m + 1], a * rows[m + 1] - b * rows[m]
        for s in range(m + 2, count):
            v, w = block[m, s], block[m + 1, s]
            upper[m, s], upper[m + 1, s] = d * v - b * w, a * w - b * v
        for q in range(m + 2, count):
            v, w = block[m, q], block[m + 1, q]
            for s in range(q, count):
                block[q, s] = block[q, s] - (v * upper[m, s] + w * upper[m + 1, s])
            rows[q] = rows[q] - (v * rows[m] + w * rows[m + 1])
    for m in range(count - 4, -1, -2):
        for s in range(m + 2, count):
            rows[m] = rows[m] - upper[m, s] * rows[s]
            rows[m + 1] = rows[m + 1] - upper[m + 1, s] * rows[s]
    return rows


def spd_inverse(matrix):
    n = matrix.shape[0]
    row = lax.broadcasted_iota(jnp.int32, (n, n), 0)
    column = lax.broadcasted_iota(jnp.int32, (n, n), 1)
    wide = jnp.concatenate([matrix, jnp.where(row == column, 1.0, 0.0).astype(F32)], axis=1)
    shape = (SUBLANES, 2 * n)
    tiles = [wide[t * SUBLANES : (t + 1) * SUBLANES, :] for t in range(n // SUBLANES)]
    sublane = lax.broadcasted_iota(jnp.int32, shape, 0)
    for k, block in enumerate(tiles):
        block = tiles[k]
        at = k * SUBLANES
        columns = [
            [jnp.broadcast_to(tile[:, at + q : at + q + 1], shape) for q in range(SUBLANES)]
            for tile in tiles
        ]
        rows = [jnp.broadcast_to(block[q : q + 1, :], shape) for q in range(SUBLANES)]
        pivot = [
            [jnp.broadcast_to(columns[k][s][q : q + 1, :], shape) for s in range(SUBLANES)]
            for q in range(SUBLANES)
        ]
        rows = solve_rows(pivot, rows)
        updated = []
        for t, tile in enumerate(tiles):
            if t == k:
                value = rows[0]
                for q in range(1, SUBLANES):
                    value = jnp.where(sublane == q, rows[q], value)
            else:
                value = tile
                for q in range(SUBLANES):
                    value = value - columns[t][q] * rows[q]
            updated.append(value)
        tiles = updated
    return jnp.concatenate([tile[:, n:] for tile in tiles], axis=0)


def inverse_kernel(*refs):
    count = (len(refs) - 1) // 2
    gram_refs, c_refs, out_ref = refs[:count], refs[count:-1], refs[-1]
    gram_c = total_of(c_refs)
    gram_b = total_of(gram_refs, 0, gram_c.shape[0])
    out_ref[...] = spd_inverse(unfold(gram_b * gram_c))


def inverse(grams_b, grams_c):
    rank = grams_c[0].shape[1] // 2
    return pl.pallas_call(
        inverse_kernel,
        out_shape=pltpu.VMEM((rank, rank), F32),
        in_specs=[VMEM] * (len(grams_b) + len(grams_c)),
        out_specs=VMEM,
        compiler_params=pltpu.CompilerParams(vmem_limit_bytes=4 << 20),
        cost_estimate=cost(4000000, 4000000),
        name="inverse",
    )(*grams_b, *grams_c)


def weigh(q_ref, factors, outs):
    row_block, rank, _ = q_ref.shape
    for tile in range(rank // SUBLANES):
        rows = pl.ds(tile * SUBLANES, SUBLANES)
        weights = [
            jnp.broadcast_to(
                factors[tile * SUBLANES : (tile + 1) * SUBLANES, i : i + 1], (SUBLANES, LANES)
            )
            for i in range(row_block)
        ]
        for out_ref, start, at, width in outs:
            for c in range(0, width, LANES):
                columns = pl.ds(pl.multiple_of(start + c, LANES), LANES)
                total = weights[0] * q_ref[0, rows, columns]
                for i in range(1, row_block):
                    total = total + weights[i] * q_ref[i, rows, columns]
                out_ref[rows, at + c : at + c + LANES] = total


def targets(q_ref, out_ref, shifts, other):
    side = lax.axis_index("ia") % 2
    side = 1 - side if other else side
    half = q_ref.shape[2] // 2
    width = half // lax.axis_size("ka")
    here = lax.axis_index("ka")
    return [
        (out_ref, side * half + (here ^ s) * width, n * width, width)
        for n, s in enumerate(shifts)
    ]


def solve_kernel(q_ref, inv_ref, *refs, shifts):
    sum_refs, (a_ref, factors_ref, send_ref) = refs[:-3], refs[-3:]
    row_block, rank, _ = q_ref.shape
    packed = total_of(sum_refs)
    columns = []
    for tile in range(rank // SUBLANES):
        group, place = divmod(tile * row_block, LANES)
        columns.append(
            packed[group * SUBLANES : (group + 1) * SUBLANES, place : place + row_block]
        )
    factors = dot(inv_ref[...], jnp.concatenate(columns, axis=0), NN)
    factors_ref[...] = factors
    weigh(q_ref, factors, targets(q_ref, send_ref, shifts, True))
    mine = lax.axis_index("ja") * lax.axis_size("ka") + lax.axis_index("ka")
    lane = lax.broadcasted_iota(jnp.int32, (rank, row_block), 1)
    chosen = jnp.where(lane == mine, factors, 0.0)
    a_ref[...] = dot(jnp.ones((SUBLANES, row_block), F32), chosen, NT)[:1, :]


def weigh_kernel(q_ref, factors_ref, out_ref, *, shifts, other):
    weigh(q_ref, factors_ref[...], targets(q_ref, out_ref, shifts, other))


def share(q, shifts):
    row_block, rank, width = q.shape
    columns = width // 2 // lax.axis_size("ka") * len(shifts)
    return (
        pltpu.VMEM((rank, columns), F32),
        cost(2 * row_block * rank * columns, 4 * row_block * rank * columns),
    )


def solve_and_weigh(q, inv, sums, shifts):
    row_block, rank, _ = q.shape
    shape, work = share(q, shifts)
    return pl.pallas_call(
        functools.partial(solve_kernel, shifts=shifts),
        out_shape=(
            jax.ShapeDtypeStruct((1, rank), F32),
            pltpu.VMEM((rank, row_block), F32),
            shape,
        ),
        in_specs=[VMEM] * (2 + len(sums)),
        out_specs=[VMEM] * 3,
        compiler_params=pltpu.CompilerParams(vmem_limit_bytes=4 << 20),
        cost_estimate=work,
        name="solve",
    )(placed_in(q, pltpu.VMEM), inv, *sums)


def weigh_columns(q, factors, shifts, other):
    shape, work = share(q, shifts)
    return pl.pallas_call(
        functools.partial(weigh_kernel, shifts=shifts, other=other),
        out_shape=shape,
        in_specs=[VMEM] * 2,
        out_specs=VMEM,
        compiler_params=pltpu.CompilerParams(vmem_limit_bytes=4 << 20),
        cost_estimate=work,
        name="weigh",
    )(placed_in(q, pltpu.VMEM), factors)


def split_kernel(kept_ref, got_ref, *out_refs):
    width = out_refs[0].shape[1]
    for n, out_ref in enumerate(out_refs):
        columns = pl.ds(n * width, width)
        out_ref[...] = kept_ref[:, columns] + got_ref[:, columns]


def split_sums(kept, got, count):
    rank, columns = kept.shape
    return pl.pallas_call(
        split_kernel,
        out_shape=[pltpu.VMEM((rank, columns // count), F32)] * count,
        in_specs=[VMEM] * 2,
        out_specs=[VMEM] * count,
        compiler_params=pltpu.CompilerParams(vmem_limit_bytes=2 << 20),
        name="split_sums",
    )(kept, got)


def final_kernel(*refs):
    part_refs, out_ref = refs[:-1], refs[-1]
    out_ref[:, 0, :] = total_of(part_refs)


def final_sum(parts):
    rank, width = parts[0].shape
    return pl.pallas_call(
        final_kernel,
        out_shape=jax.ShapeDtypeStruct((rank, 1, width), F32),
        in_specs=[VMEM] * len(parts),
        out_specs=VMEM,
        compiler_params=pltpu.CompilerParams(vmem_limit_bytes=2 << 20),
        name="final_sum",
    )(*parts)


def swap(x, axis, s):
    n = lax.axis_size(axis)
    return lax.ppermute(x, axis, [(i, i ^ s) for i in range(n)])


def swaps(x, axis):
    n = lax.axis_size(axis)
    return [x] + [swap(x, axis, s) for s in range(1, n)]


def body(tensor, factor_b, factor_c):
    row_block, _, width = tensor.shape
    rank = factor_c.shape[1]
    n_ia, n_ka = lax.axis_size("ia"), lax.axis_size("ka")
    lines = row_block * rank // LANES
    parts = swaps(factor_b.T, "ka")
    q, gram_c = contract(tensor, factor_c)
    grams_c = swaps(gram_c, "ka")
    sums = swaps(mode_one_sums(q, parts), "ja")
    tails = swaps(add_tail(sums, lines), "ka")
    inv = inverse(sums, grams_c)
    far = list(reversed(range(2, n_ka)))
    near = [1, 0]
    if n_ia == 2 and width % (n_ia * n_ka * LANES) == 0:
        a_row, factors, send = solve_and_weigh(q, inv, tails, far)
        got = swap(send, "ia", 1)
        send_near = weigh_columns(q, factors, near, True)
        got_near = swap(send_near, "ia", 1)
        kept = weigh_columns(q, factors, far, False)
        kept_near = weigh_columns(q, factors, near, False)
        pieces = split_sums(kept, got, len(far))
        final = [swap(piece, "ka", s) for piece, s in zip(pieces, far)]
        next_piece, own = split_sums(kept_near, got_near, len(near))
        final.append(swap(next_piece, "ka", 1))
        return a_row, final_sum([own] + final[::-1])
    a_row, factors, _ = solve_and_weigh(q, inv, tails, near)
    whole = jnp.einsum("irj,ri->rj", q, factors, precision=HIGHEST)
    reduced = lax.psum_scatter(whole, ("ia", "ka"), scatter_dimension=1, tiled=True)
    return a_row, reduced.reshape(rank, 1, reduced.shape[1])


def solution(mesh):
    placed = (P("ia", "ka", "ja"), P(("ja", "ka"), None), P("ka", None))
    return jax.shard_map(
        body,
        mesh=mesh,
        in_specs=placed,
        out_specs=(P(("ia", "ja", "ka"), None), P(None, "ja", ("ia", "ka"))),
        check_vma=False,
    )
```

profile of v0, /device:TPU:0, one launch (start us, length us, event | category | flops | bytes accessed | tf_op | source)
XLA Modules:
  0.0 45.9 jit_solution(2221238900350862525)
XLA Ops:
  0.6 0.0 copy-start
  0.6 5.1 %collective-permute-start = (f32[64,512]{1,0:T(8,128)}, f32[64,512]{1,0:T(8,128)S(1)}, u32[]{:S(2)}, u32[]{:S(2)}) collective-permute-start(f32[64,512]{1,0:T(8,128)} %bitcast.1), channel_id=1, source_target_pairs={{0,3},{1,2},{2,1},{3,0},{4,7},{5,6},{6,5},{7,4},{8,11},{9,10},{10,... | collective-permute-start | bytes 393224 | tf_op jit(solution)/shard_map/ppermute | solution.py:433
  5.8 0.0 collective-permute-start.1
  5.8 0.6 %collective-permute-start.2 = (f32[64,512]{1,0:T(8,128)}, f32[64,512]{1,0:T(8,128)S(1)}, u32[]{:S(2)}, u32[]{:S(2)}) collective-permute-start(f32[64,512]{1,0:T(8,128)} %bitcast.3), channel_id=1, source_target_pairs={{0,1},{1,0},{2,3},{3,2},{4,5},{5,4},{6,7},{7,6},{8,9},{9,8},{10,11... | collective-permute-start | bytes 393224 | tf_op jit(solution)/shard_map/ppermute | solution.py:433
  6.4 6.3 %contract.1 = (f32[16,64,2048]{2,1,0:T(8,128)S(1)}, f32[32,128]{1,0:T(8,128)S(1)}) custom-call(f32[16,64,2048]{2,1,0:T(8,128)} %x_hbm.1, f32[64,64]{1,0:T(8,128)} %c_hbm.1), custom_call_target="tpu_custom_call" | custom-call | flops 1073741824 | bytes 8388608 | tf_op jit(solution)/shard_map/contract/pallas_call | solution.py:87
  12.8 0.0 collective-permute-done.refs_1_
  12.8 0.0 copy-done
  12.8 0.9 %mode_one_early.1 = (f32[1024,128]{1,0:T(8,128)S(1)}, f32[32,128]{1,0:T(8,128)S(1)}) custom-call(f32[16,64,2048]{2,1,0:T(8,128)S(1)} %get-tuple-element.13.q_ref, f32[64,512]{1,0:T(8,128)S(1)} %bitcast.4, f32[64,512]{1,0:T(8,128)S(1)} %collective-permute-done.refs_1_), custom_call_target="tpu_custom_call" | custom-call | flops 2097152 | bytes 4194304 | tf_op jit(solution)/shard_map/mode_one_early/pallas_call | solution.py:180
  13.7 3.4 %collective-permute-done.1.refs_0_ = f32[64,512]{1,0:T(8,128)S(1)} collective-permute-done((f32[64,512]{1,0:T(8,128)}, f32[64,512]{1,0:T(8,128)S(1)}, u32[]{:S(2)}, u32[]{:S(2)}) %collective-permute-start.1) | collective-permute-done | bytes 131104 | tf_op jit(solution)/shard_map/ppermute | solution.py:433
  17.1 0.0 collective-permute-done.2.refs_1_
  17.1 0.8 %mode_one_late.1.refs_0_ = f32[40,128]{1,0:T(8,128)S(1)} custom-call(f32[16,64,2048]{2,1,0:T(8,128)S(1)} %get-tuple-element.13.q_ref, f32[1024,128]{1,0:T(8,128)S(1)} %get-tuple-element.14.sums_ref, f32[32,128]{1,0:T(8,128)S(1)} %get-tuple-element.15.gram_ref, f32[64,512]{1,0:T(8,128)S(1)} %collective-permute-done.1.refs_0_, ...), custom_call_target="tpu_custom_call" | custom-call | flops 2097152 | bytes 4194304 | tf_op jit(solution)/shard_map/mode_one_late/pallas_call | solution.py:192
  17.9 0.1 collective-permute-start.3
  18.0 1.6 %collective-permute-start.4 = (f32[40,128]{1,0:T(8,128)S(1)}, f32[40,128]{1,0:T(8,128)S(1)}, u32[]{:S(2)}, u32[]{:S(2)}) collective-permute-start(f32[40,128]{1,0:T(8,128)S(1)} %mode_one_late.1.refs_0_), channel_id=1, source_target_pairs={{0,8},{4,12},{8,0},{12,4},{1,9},{5,13},{9,1},{13,5},{2,10},{6,14},... | collective-permute-start | bytes 61448 | tf_op jit(solution)/shard_map/ppermute | solution.py:433
  19.5 0.3 collective-permute-start.5
  19.8 0.0 collective-permute-start.6
  19.8 3.0 %collective-permute-start.7 = (f32[32,128]{1,0:T(8,128)S(1)}, f32[32,128]{1,0:T(8,128)S(1)}, u32[]{:S(2)}, u32[]{:S(2)}) collective-permute-start(f32[32,128]{1,0:T(8,128)S(1)} %get-tuple-element.16.refs_4_), channel_id=1, source_target_pairs={{0,2},{1,3},{2,0},{3,1},{4,6},{5,7},{6,4},{7,5},{8,10},{9,11},{10,... | collective-permute-start | bytes 49160 | tf_op jit(solution)/shard_map/ppermute | solution.py:433
  22.9 0.0 collective-permute-done.3.refs_1_
  22.9 1.3 %collective-permute-start.8 = (f32[32,128]{1,0:T(8,128)S(1)}, f32[32,128]{1,0:T(8,128)S(1)}, u32[]{:S(2)}, u32[]{:S(2)}) collective-permute-start(f32[32,128]{1,0:T(8,128)S(1)} %get-tuple-element.16.refs_4_), channel_id=1, source_target_pairs={{0,3},{1,2},{2,1},{3,0},{4,7},{5,6},{6,5},{7,4},{8,11},{9,10},{10,... | collective-permute-start | bytes 49160 | tf_op jit(solution)/shard_map/ppermute | solution.py:433
  24.2 0.0 collective-permute-done.4.refs_2_
  24.2 0.0 collective-permute-done.5.refs_3_
  24.2 0.2 collective-permute-start.10
  24.4 2.4 %collective-permute-start.11 = (f32[8,128]{1,0:T(8,128)S(1)}, f32[8,128]{1,0:T(8,128)S(1)}, u32[]{:S(2)}, u32[]{:S(2)}) collective-permute-start(f32[8,128]{1,0:T(8,128)S(1)} %add_tail.1.refs_0_), channel_id=1, source_target_pairs={{0,3},{1,2},{2,1},{3,0},{4,7},{5,6},{6,5},{7,4},{8,11},{9,10},{10,... | collective-permute-start | bytes 12296 | tf_op jit(solution)/shard_map/ppermute | solution.py:433
  26.8 0.0 collective-permute-done.6.refs_5_
  26.8 0.9 %collective-permute-start.9 = (f32[8,128]{1,0:T(8,128)S(1)}, f32[8,128]{1,0:T(8,128)S(1)}, u32[]{:S(2)}, u32[]{:S(2)}) collective-permute-start(f32[8,128]{1,0:T(8,128)S(1)} %add_tail.1.refs_0_), channel_id=1, source_target_pairs={{0,1},{1,0},{2,3},{3,2},{4,5},{5,4},{6,7},{7,6},{8,9},{9,8},{10,11... | collective-permute-start | bytes 12296 | tf_op jit(solution)/shard_map/ppermute | solution.py:433
  27.8 0.0 collective-permute-done.7.refs_6_
  27.8 0.7 %collective-permute-done.8.refs_7_ = f32[32,128]{1,0:T(8,128)S(1)} collective-permute-done((f32[32,128]{1,0:T(8,128)S(1)}, f32[32,128]{1,0:T(8,128)S(1)}, u32[]{:S(2)}, u32[]{:S(2)}) %collective-permute-start.8) | collective-permute-done | bytes 16416 | tf_op jit(solution)/shard_map/ppermute | solution.py:433
  28.4 2.1 %inverse.1.inv_ref = f32[64,64]{1,0:T(8,128)S(1)} custom-call(f32[40,128]{1,0:T(8,128)S(1)} %mode_one_late.1.refs_0_, f32[40,128]{1,0:T(8,128)S(1)} %collective-permute-done.3.refs_1_, f32[40,128]{1,0:T(8,128)S(1)} %collective-permute-done.4.refs_2_, f32[40,128]{1,0:T(8,128)S(1)} %collective-permute-done.5.refs_3_, f32[32,128]{1,0:T(8,128)S(1)} %get-tuple-element.16.refs_4_, ...), custom_call_target="tpu_custom_call" | custom-call | flops 4000000 | bytes 4000000 | tf_op jit(solution)/shard_map/inverse/pallas_call | solution.py:290
  30.6 0.0 collective-permute-done.10.refs_2_
  30.6 0.0 collective-permute-done.11.refs_3_
  30.6 0.0 collective-permute-done.9.refs_1_
  30.6 1.0 %solve.1 = (f32[1,64]{1,0:T(1,128)}, f32[64,16]{1,0:T(8,128)S(1)}, f32[64,512]{1,0:T(8,128)S(1)}) custom-call(f32[16,64,2048]{2,1,0:T(8,128)S(1)} %get-tuple-element.13.q_ref, f32[64,64]{1,0:T(8,128)S(1)} %inverse.1.inv_ref, f32[8,128]{1,0:T(8,128)S(1)} %add_tail.1.refs_0_, f32[8,128]{1,0:T(8,128)S(1)} %collective-permute-done.9.refs_1_, ...), custom_call_target="tpu_custom_call" | custom-call | flops 1048576 | bytes 2097152 | tf_op jit(solution)/shard_map/solve/pallas_call | solution.py:367
  31.6 1.5 %collective-permute-start.14 = (f32[64,512]{1,0:T(8,128)S(1)}, f32[64,512]{1,0:T(8,128)S(1)}, u32[]{:S(2)}, u32[]{:S(2)}) collective-permute-start(f32[64,512]{1,0:T(8,128)S(1)} %get-tuple-element.21), channel_id=1, source_target_pairs={{0,16},{16,0},{1,17},{17,1},{2,18},{18,2},{3,19},{19,3},{4,20},{20... | collective-permute-start | bytes 393224 | tf_op jit(solution)/shard_map/ppermute | solution.py:433
  33.1 0.4 weigh.4
  33.4 0.6 %collective-permute-start.12 = (f32[64,512]{1,0:T(8,128)S(1)}, f32[64,512]{1,0:T(8,128)S(1)}, u32[]{:S(2)}, u32[]{:S(2)}) collective-permute-start(f32[64,512]{1,0:T(8,128)S(1)} %weigh.4), channel_id=1, source_target_pairs={{0,16},{16,0},{1,17},{17,1},{2,18},{18,2},{3,19},{19,3},{4,20},{20... | collective-permute-start | bytes 393224 | tf_op jit(solution)/shard_map/ppermute | solution.py:433
  34.0 0.4 weigh.5.kept_ref
  34.4 0.4 weigh.3.kept_ref
  34.8 2.5 %collective-permute-done.14.got_ref = f32[64,512]{1,0:T(8,128)S(1)} collective-permute-done((f32[64,512]{1,0:T(8,128)S(1)}, f32[64,512]{1,0:T(8,128)S(1)}, u32[]{:S(2)}, u32[]{:S(2)}) %collective-permute-start.14) | collective-permute-done | bytes 131104 | tf_op jit(solution)/shard_map/ppermute | solution.py:433
  37.3 1.2 %collective-permute-start.15 = (f32[64,256]{1,0:T(8,128)S(1)}, f32[64,256]{1,0:T(8,128)S(1)}, u32[]{:S(2)}, u32[]{:S(2)}) collective-permute-start(f32[64,256]{1,0:T(8,128)S(1)} %get-tuple-element.22), channel_id=1, source_target_pairs={{0,2},{1,3},{2,0},{3,1},{4,6},{5,7},{6,4},{7,5},{8,10},{9,11},{10,... | collective-permute-start | bytes 196616 | tf_op jit(solution)/shard_map/ppermute | solution.py:433
  38.4 2.1 %collective-permute-start.16 = (f32[64,256]{1,0:T(8,128)S(1)}, f32[64,256]{1,0:T(8,128)S(1)}, u32[]{:S(2)}, u32[]{:S(2)}) collective-permute-start(f32[64,256]{1,0:T(8,128)S(1)} %get-tuple-element.23), channel_id=1, source_target_pairs={{0,3},{1,2},{2,1},{3,0},{4,7},{5,6},{6,5},{7,4},{8,11},{9,10},{10,... | collective-permute-start | bytes 196616 | tf_op jit(solution)/shard_map/ppermute | solution.py:433
  40.5 0.0 collective-permute-done.12.got_ref
  40.5 0.4 collective-permute-start.13
  40.9 2.3 %collective-permute-done.15.refs_2_ = f32[64,256]{1,0:T(8,128)S(1)} collective-permute-done((f32[64,256]{1,0:T(8,128)S(1)}, f32[64,256]{1,0:T(8,128)S(1)}, u32[]{:S(2)}, u32[]{:S(2)}) %collective-permute-start.15) | collective-permute-done | bytes 65568 | tf_op jit(solution)/shard_map/ppermute | solution.py:433
  43.2 1.4 %collective-permute-done.16.refs_3_ = f32[64,256]{1,0:T(8,128)S(1)} collective-permute-done((f32[64,256]{1,0:T(8,128)S(1)}, f32[64,256]{1,0:T(8,128)S(1)}, u32[]{:S(2)}, u32[]{:S(2)}) %collective-permute-start.16) | collective-permute-done | bytes 65568 | tf_op jit(solution)/shard_map/ppermute | solution.py:433
  44.6 0.7 %collective-permute-done.13.refs_1_ = f32[64,256]{1,0:T(8,128)S(1)} collective-permute-done((f32[64,256]{1,0:T(8,128)S(1)}, f32[64,256]{1,0:T(8,128)S(1)}, u32[]{:S(2)}, u32[]{:S(2)}) %collective-permute-start.13) | collective-permute-done | bytes 65568 | tf_op jit(solution)/shard_map/ppermute | solution.py:433
  45.3 0.7 %final_sum.1 = f32[64,1,256]{2,1,0:T(1,128)} custom-call(f32[64,256]{1,0:T(8,128)S(1)} %get-tuple-element.19.refs_0_, f32[64,256]{1,0:T(8,128)S(1)} %collective-permute-done.13.refs_1_, f32[64,256]{1,0:T(8,128)S(1)} %collective-permute-done.15.refs_2_, f32[64,256]{1,0:T(8,128)S(1)} %collective-permute-done.16.refs_3_), custom_call_target="tpu_custom_call" | custom-call | tf_op jit(solution)/shard_map/final_sum/pallas_call | solution.py:421
  (3 shorter events, 0.0 us)
Async XLA Ops:
  0.6 12.2 %copy-start = (f32[512,64]{0,1:T(8,128)S(1)}, f32[512,64]{0,1:T(8,128)}, u32[]{:S(2)}) copy-start(f32[512,64]{0,1:T(8,128)} %param.4) | copy-start | bytes 393220
  0.6 12.1 %collective-permute-start = (f32[64,512]{1,0:T(8,128)}, f32[64,512]{1,0:T(8,128)S(1)}, u32[]{:S(2)}, u32[]{:S(2)}) collective-permute-start(f32[64,512]{1,0:T(8,128)} %bitcast.1), channel_id=1, source_target_pairs={{0,3},{1,2},{2,1},{3,0},{4,7},{5,6},{6,5},{7,4},{8,11},{9,10},{10,... | collective-permute-start | bytes 393224 | tf_op jit(solution)/shard_map/ppermute | solution.py:433
  5.8 11.3 %collective-permute-start.1 = (f32[64,512]{1,0:T(8,128)}, f32[64,512]{1,0:T(8,128)S(1)}, u32[]{:S(2)}, u32[]{:S(2)}) collective-permute-start(f32[64,512]{1,0:T(8,128)} %bitcast.2), channel_id=1, source_target_pairs={{0,2},{1,3},{2,0},{3,1},{4,6},{5,7},{6,4},{7,5},{8,10},{9,11},{10,... | collective-permute-start | bytes 393224 | tf_op jit(solution)/shard_map/ppermute | solution.py:433
  5.8 11.3 %collective-permute-start.2 = (f32[64,512]{1,0:T(8,128)}, f32[64,512]{1,0:T(8,128)S(1)}, u32[]{:S(2)}, u32[]{:S(2)}) collective-permute-start(f32[64,512]{1,0:T(8,128)} %bitcast.3), channel_id=1, source_target_pairs={{0,1},{1,0},{2,3},{3,2},{4,5},{5,4},{6,7},{7,6},{8,9},{9,8},{10,11... | collective-permute-start | bytes 393224 | tf_op jit(solution)/shard_map/ppermute | solution.py:433
  17.9 5.0 %collective-permute-start.3 = (f32[40,128]{1,0:T(8,128)S(1)}, f32[40,128]{1,0:T(8,128)S(1)}, u32[]{:S(2)}, u32[]{:S(2)}) collective-permute-start(f32[40,128]{1,0:T(8,128)S(1)} %mode_one_late.1.refs_0_), channel_id=1, source_target_pairs={{0,4},{4,0},{8,12},{12,8},{1,5},{5,1},{9,13},{13,9},{2,6},{6,2},{1... | collective-permute-start | bytes 61448 | tf_op jit(solution)/shard_map/ppermute | solution.py:433
  18.0 6.2 %collective-permute-start.4 = (f32[40,128]{1,0:T(8,128)S(1)}, f32[40,128]{1,0:T(8,128)S(1)}, u32[]{:S(2)}, u32[]{:S(2)}) collective-permute-start(f32[40,128]{1,0:T(8,128)S(1)} %mode_one_late.1.refs_0_), channel_id=1, source_target_pairs={{0,8},{4,12},{8,0},{12,4},{1,9},{5,13},{9,1},{13,5},{2,10},{6,14},... | collective-permute-start | bytes 61448 | tf_op jit(solution)/shard_map/ppermute | solution.py:433
  19.5 4.7 %collective-permute-start.5 = (f32[40,128]{1,0:T(8,128)S(1)}, f32[40,128]{1,0:T(8,128)S(1)}, u32[]{:S(2)}, u32[]{:S(2)}) collective-permute-start(f32[40,128]{1,0:T(8,128)S(1)} %mode_one_late.1.refs_0_), channel_id=1, source_target_pairs={{0,12},{4,8},{8,4},{12,0},{1,13},{5,9},{9,5},{13,1},{2,14},{6,10},... | collective-permute-start | bytes 61448 | tf_op jit(solution)/shard_map/ppermute | solution.py:433
  19.8 7.0 %collective-permute-start.6 = (f32[32,128]{1,0:T(8,128)S(1)}, f32[32,128]{1,0:T(8,128)S(1)}, u32[]{:S(2)}, u32[]{:S(2)}) collective-permute-start(f32[32,128]{1,0:T(8,128)S(1)} %get-tuple-element.16.refs_4_), channel_id=1, source_target_pairs={{0,1},{1,0},{2,3},{3,2},{4,5},{5,4},{6,7},{7,6},{8,9},{9,8},{10,11... | collective-permute-start | bytes 49160 | tf_op jit(solution)/shard_map/ppermute | solution.py:433
  19.8 8.0 %collective-permute-start.7 = (f32[32,128]{1,0:T(8,128)S(1)}, f32[32,128]{1,0:T(8,128)S(1)}, u32[]{:S(2)}, u32[]{:S(2)}) collective-permute-start(f32[32,128]{1,0:T(8,128)S(1)} %get-tuple-element.16.refs_4_), channel_id=1, source_target_pairs={{0,2},{1,3},{2,0},{3,1},{4,6},{5,7},{6,4},{7,5},{8,10},{9,11},{10,... | collective-permute-start | bytes 49160 | tf_op jit(solution)/shard_map/ppermute | solution.py:433
  22.9 5.6 %collective-permute-start.8 = (f32[32,128]{1,0:T(8,128)S(1)}, f32[32,128]{1,0:T(8,128)S(1)}, u32[]{:S(2)}, u32[]{:S(2)}) collective-permute-start(f32[32,128]{1,0:T(8,128)S(1)} %get-tuple-element.16.refs_4_), channel_id=1, source_target_pairs={{0,3},{1,2},{2,1},{3,0},{4,7},{5,6},{6,5},{7,4},{8,11},{9,10},{10,... | collective-permute-start | bytes 49160 | tf_op jit(solution)/shard_map/ppermute | solution.py:433
  24.2 6.3 %collective-permute-start.10 = (f32[8,128]{1,0:T(8,128)S(1)}, f32[8,128]{1,0:T(8,128)S(1)}, u32[]{:S(2)}, u32[]{:S(2)}) collective-permute-start(f32[8,128]{1,0:T(8,128)S(1)} %add_tail.1.refs_0_), channel_id=1, source_target_pairs={{0,2},{1,3},{2,0},{3,1},{4,6},{5,7},{6,4},{7,5},{8,10},{9,11},{10,... | collective-permute-start | bytes 12296 | tf_op jit(solution)/shard_map/ppermute | solution.py:433
  24.4 6.2 %collective-permute-start.11 = (f32[8,128]{1,0:T(8,128)S(1)}, f32[8,128]{1,0:T(8,128)S(1)}, u32[]{:S(2)}, u32[]{:S(2)}) collective-permute-start(f32[8,128]{1,0:T(8,128)S(1)} %add_tail.1.refs_0_), channel_id=1, source_target_pairs={{0,3},{1,2},{2,1},{3,0},{4,7},{5,6},{6,5},{7,4},{8,11},{9,10},{10,... | collective-permute-start | bytes 12296 | tf_op jit(solution)/shard_map/ppermute | solution.py:433
  26.8 3.7 %collective-permute-start.9 = (f32[8,128]{1,0:T(8,128)S(1)}, f32[8,128]{1,0:T(8,128)S(1)}, u32[]{:S(2)}, u32[]{:S(2)}) collective-permute-start(f32[8,128]{1,0:T(8,128)S(1)} %add_tail.1.refs_0_), channel_id=1, source_target_pairs={{0,1},{1,0},{2,3},{3,2},{4,5},{5,4},{6,7},{7,6},{8,9},{9,8},{10,11... | collective-permute-start | bytes 12296 | tf_op jit(solution)/shard_map/ppermute | solution.py:433
  31.6 5.7 %collective-permute-start.14 = (f32[64,512]{1,0:T(8,128)S(1)}, f32[64,512]{1,0:T(8,128)S(1)}, u32[]{:S(2)}, u32[]{:S(2)}) collective-permute-start(f32[64,512]{1,0:T(8,128)S(1)} %get-tuple-element.21), channel_id=1, source_target_pairs={{0,16},{16,0},{1,17},{17,1},{2,18},{18,2},{3,19},{19,3},{4,20},{20... | collective-permute-start | bytes 393224 | tf_op jit(solution)/shard_map/ppermute | solution.py:433
  33.4 7.0 %collective-permute-start.12 = (f32[64,512]{1,0:T(8,128)S(1)}, f32[64,512]{1,0:T(8,128)S(1)}, u32[]{:S(2)}, u32[]{:S(2)}) collective-permute-start(f32[64,512]{1,0:T(8,128)S(1)} %weigh.4), channel_id=1, source_target_pairs={{0,16},{16,0},{1,17},{17,1},{2,18},{18,2},{3,19},{19,3},{4,20},{20... | collective-permute-start | bytes 393224 | tf_op jit(solution)/shard_map/ppermute | solution.py:433
  37.3 5.9 %collective-permute-start.15 = (f32[64,256]{1,0:T(8,128)S(1)}, f32[64,256]{1,0:T(8,128)S(1)}, u32[]{:S(2)}, u32[]{:S(2)}) collective-permute-start(f32[64,256]{1,0:T(8,128)S(1)} %get-tuple-element.22), channel_id=1, source_target_pairs={{0,2},{1,3},{2,0},{3,1},{4,6},{5,7},{6,4},{7,5},{8,10},{9,11},{10,... | collective-permute-start | bytes 196616 | tf_op jit(solution)/shard_map/ppermute | solution.py:433
  38.4 6.2 %collective-permute-start.16 = (f32[64,256]{1,0:T(8,128)S(1)}, f32[64,256]{1,0:T(8,128)S(1)}, u32[]{:S(2)}, u32[]{:S(2)}) collective-permute-start(f32[64,256]{1,0:T(8,128)S(1)} %get-tuple-element.23), channel_id=1, source_target_pairs={{0,3},{1,2},{2,1},{3,0},{4,7},{5,6},{6,5},{7,4},{8,11},{9,10},{10,... | collective-permute-start | bytes 196616 | tf_op jit(solution)/shard_map/ppermute | solution.py:433
  40.5 4.8 %collective-permute-start.13 = (f32[64,256]{1,0:T(8,128)S(1)}, f32[64,256]{1,0:T(8,128)S(1)}, u32[]{:S(2)}, u32[]{:S(2)}) collective-permute-start(f32[64,256]{1,0:T(8,128)S(1)} %get-tuple-element.20), channel_id=1, source_target_pairs={{0,1},{1,0},{2,3},{3,2},{4,5},{5,4},{6,7},{7,6},{8,9},{9,8},{10,11... | collective-permute-start | bytes 196616 | tf_op jit(solution)/shard_map/ppermute | solution.py:433
where the time goes:
time: 46.1 us; the launch traced here: 45.9 us
  starting transfers between devices  21.4 us (46%)
  Pallas kernels  12.9 us (28%)
  waiting for transfers between devices  10.9 us (24%)
  between operations  0.74 us (2%)
    ppermute x17, starting transfers between devices, swap(): return lax.ppermute(x, axis, [(i, i ^ s) for i in range(n)])  21.4 us
    ppermute x17, waiting for transfers between devices, swap(): return lax.ppermute(x, axis, [(i, i ^ s) for i in range(n)])  10.9 us
    pallas_call x1, Pallas kernels, contract(): pl.pallas_call(functools.partial(contract_kernel, chunks=chunks), out_sha...  6.35 us
    pallas_call x1, Pallas kernels, inverse(): pl.pallas_call(inverse_kernel, out_shape=pltpu.VMEM((rank, rank), F32), i...  2.13 us
    pallas_call x3, Pallas kernels, weigh_columns(): pl.pallas_call(functools.partial(weigh_kernel, shifts=shifts, other=other...  1.09 us
    pallas_call x1, Pallas kernels, solve_and_weigh(): pl.pallas_call(functools.partial(solve_kernel, shifts=shifts), out_shape=...  0.97 us
  transfers between devices with their start and end apart: 17, of which 6 were waited for; matrix products, arithmetic and copies ran while one was open for 0% of the time, Pallas kernels for 23%

commit v1 on v0

--- a/solution.py
+++ b/solution.py
@@ -50,22 +50,26 @@
 
 
 def contract_kernel(
-    x_hbm, c_hbm, q_ref, gram_ref, x_ref, c_ref, lhs_ref, x_sems, c_sem, *, chunks
+    x_hbm, b_hbm, c_hbm, q_ref, gram_b_ref, gram_c_ref, x_ref, b_ref, c_ref, lhs_ref, sems, *, chunks
 ):
     rows = q_ref.shape[0] // chunks
     copies = [
         pltpu.make_async_copy(
-            x_hbm.at[pl.ds(n * rows, rows)], x_ref.at[pl.ds(n * rows, rows)], x_sems.at[n]
+            x_hbm.at[pl.ds(n * rows, rows)], x_ref.at[pl.ds(n * rows, rows)], sems.at[n]
         )
         for n in range(chunks)
     ]
-    c_copy = pltpu.make_async_copy(c_hbm, c_ref, c_sem)
+    c_copy = pltpu.make_async_copy(c_hbm, c_ref, sems.at[chunks])
+    b_copy = pltpu.make_async_copy(b_hbm, b_ref, sems.at[chunks + 1])
     c_copy.start()
+    b_copy.start()
     for copy in copies:
         copy.start()
     c_copy.wait()
+    b_copy.wait()
     c = c_ref[...]
-    gram_ref[...] = fold(dot(c, c, TN))
+    gram_c_ref[...] = fold(dot(c, c, TN))
+    gram_b_ref[...] = fold(gram_terms([b_ref], b_ref.shape[0]))
     ct = c.T
     high = ct.astype(BF16)
     low = (ct - high.astype(F32)).astype(BF16)
@@ -80,7 +84,7 @@
             q_ref[i] = jnp.dot(lhs_ref[...], rhs, preferred_element_type=F32)
 
 
-def contract(tensor, factor_c):
+def contract(tensor, bt, factor_c):
     row_block, depth, width = tensor.shape
     rank = factor_c.shape[1]
     chunks = 4
@@ -89,20 +93,21 @@
         out_shape=(
             pltpu.VMEM((row_block, rank, width), F32),
             pltpu.VMEM((rank // 2, 2 * rank), F32),
+            pltpu.VMEM((rank // 2, 2 * rank), F32),
         ),
-        in_specs=[HBM, HBM],
-        out_specs=[VMEM, VMEM],
+        in_specs=[HBM] * 3,
+        out_specs=[VMEM] * 3,
         scratch_shapes=[
             pltpu.VMEM(tensor.shape, F32),
+            pltpu.VMEM(bt.shape, F32),
             pltpu.VMEM(factor_c.shape, F32),
             pltpu.VMEM((rank, 4 * depth), BF16),
-            pltpu.SemaphoreType.DMA((chunks,)),
-            pltpu.SemaphoreType.DMA,
+            pltpu.SemaphoreType.DMA((chunks + 2,)),
         ],
         compiler_params=pltpu.CompilerParams(vmem_limit_bytes=12 << 20),
         cost_estimate=cost(8 * row_block * depth * rank * width, 4 * row_block * depth * width),
         name="contract",
-    )(placed_in(tensor, pltpu.HBM), placed_in(factor_c, pltpu.HBM))
+    )(*(placed_in(x, pltpu.HBM) for x in (tensor, bt, factor_c)))
 
 
 def gram_terms(part_refs, rank):
@@ -137,10 +142,11 @@
             yield tile, i, total
 
 
-def early_kernel(q_ref, *refs, shifts):
+def early_kernel(q_ref, own_ref, *refs, shifts):
     part_refs, (sums_ref, gram_ref) = refs[:-2], refs[-2:]
     row_block, rank, _ = q_ref.shape
-    gram_ref[...] = fold(gram_terms(part_refs, rank))
+    others = [part for s, part in zip(shifts, part_refs) if s != 0]
+    gram_ref[...] = fold(gram_terms(others, rank)) + own_ref[...]
     for tile, i, total in weighted_sums(q_ref, part_refs, shifts):
         at = (tile * row_block + i) * SUBLANES
         sums_ref[at : at + SUBLANES, :] = total
@@ -167,7 +173,7 @@
     out_ref[:half, :] = gram + gram_ref[...]
 
 
-def mode_one_sums(q, parts):
+def mode_one_sums(q, own_gram, parts):
     row_block, rank, width = q.shape
     lines = row_block * rank // LANES
     count = len(parts)
@@ -183,12 +189,12 @@
             pltpu.VMEM((row_block * rank, LANES), F32),
             pltpu.VMEM((rank // 2, 2 * rank), F32),
         ),
-        in_specs=[VMEM] * (1 + len(early)),
+        in_specs=[VMEM] * (2 + len(early)),
         out_specs=[VMEM] * 2,
         compiler_params=params,
         cost_estimate=work,
         name="mode_one_early",
-    )(q, *[parts[s] for s in early])
+    )(q, own_gram, *[parts[s] for s in early])
     return pl.pallas_call(
         functools.partial(late_kernel, shifts=late),
         out_shape=pltpu.VMEM((rank // 2 + lines, LANES), F32),
@@ -330,7 +336,7 @@
 
 
 def solve_kernel(q_ref, inv_ref, *refs, shifts):
-    sum_refs, (a_ref, factors_ref, send_ref) = refs[:-3], refs[-3:]
+    sum_refs, (factors_ref, send_ref) = refs[:-2], refs[-2:]
     row_block, rank, _ = q_ref.shape
     packed = total_of(sum_refs)
     columns = []
@@ -342,10 +348,25 @@
     factors = dot(inv_ref[...], jnp.concatenate(columns, axis=0), NN)
     factors_ref[...] = factors
     weigh(q_ref, factors, targets(q_ref, send_ref, shifts, True))
+
+
+def row_kernel(factors_ref, out_ref):
+    factors = factors_ref[...]
     mine = lax.axis_index("ja") * lax.axis_size("ka") + lax.axis_index("ka")
-    lane = lax.broadcasted_iota(jnp.int32, (rank, row_block), 1)
+    lane = lax.broadcasted_iota(jnp.int32, factors.shape, 1)
     chosen = jnp.where(lane == mine, factors, 0.0)
-    a_ref[...] = dot(jnp.ones((SUBLANES, row_block), F32), chosen, NT)[:1, :]
+    out_ref[...] = dot(jnp.ones((SUBLANES, factors.shape[1]), F32), chosen, NT)[:1, :]
+
+
+def own_row(factors):
+    return pl.pallas_call(
+        row_kernel,
+        out_shape=jax.ShapeDtypeStruct((1, factors.shape[0]), F32),
+        in_specs=[VMEM],
+        out_specs=VMEM,
+        compiler_params=pltpu.CompilerParams(vmem_limit_bytes=2 << 20),
+        name="own_row",
+    )(factors)
 
 
 def weigh_kernel(q_ref, factors_ref, out_ref, *, shifts, other):
@@ -366,13 +387,9 @@
     shape, work = share(q, shifts)
     return pl.pallas_call(
         functools.partial(solve_kernel, shifts=shifts),
-        out_shape=(
-            jax.ShapeDtypeStruct((1, rank), F32),
-            pltpu.VMEM((rank, row_block), F32),
-            shape,
-        ),
+        out_shape=(pltpu.VMEM((rank, row_block), F32), shape),
         in_specs=[VMEM] * (2 + len(sums)),
-        out_specs=[VMEM] * 3,
+        out_specs=[VMEM] * 2,
         compiler_params=pltpu.CompilerParams(vmem_limit_bytes=4 << 20),
         cost_estimate=work,
         name="solve",
@@ -443,30 +460,37 @@
     rank = factor_c.shape[1]
     n_ia, n_ka = lax.axis_size("ia"), lax.axis_size("ka")
     lines = row_block * rank // LANES
-    parts = swaps(factor_b.T, "ka")
-    q, gram_c = contract(tensor, factor_c)
+    bt = factor_b.T
+    parts = swaps(bt, "ka")
+    q, own_gram, gram_c = contract(tensor, bt, factor_c)
     grams_c = swaps(gram_c, "ka")
-    sums = swaps(mode_one_sums(q, parts), "ja")
+    sums = swaps(mode_one_sums(q, own_gram, parts), "ja")
     tails = swaps(add_tail(sums, lines), "ka")
     inv = inverse(sums, grams_c)
-    far = list(reversed(range(2, n_ka)))
-    near = [1, 0]
     if n_ia == 2 and width % (n_ia * n_ka * LANES) == 0:
-        a_row, factors, send = solve_and_weigh(q, inv, tails, far)
-        got = swap(send, "ia", 1)
-        send_near = weigh_columns(q, factors, near, True)
-        got_near = swap(send_near, "ia", 1)
-        kept = weigh_columns(q, factors, far, False)
-        kept_near = weigh_columns(q, factors, near, False)
-        pieces = split_sums(kept, got, len(far))
-        final = [swap(piece, "ka", s) for piece, s in zip(pieces, far)]
-        next_piece, own = split_sums(kept_near, got_near, len(near))
-        final.append(swap(next_piece, "ka", 1))
-        return a_row, final_sum([own] + final[::-1])
-    a_row, factors, _ = solve_and_weigh(q, inv, tails, near)
+        groups = chunks_of(n_ka)
+        factors, sent = solve_and_weigh(q, inv, tails, groups[0])
+        got = [swap(sent, "ia", 1)]
+        for n, group in enumerate(groups[1:], 1):
+            sent = weigh_columns(q, factors, group, True)
+            got.append(swap(sent, "ia", 1))
+        final = []
+        for n, group in enumerate(groups):
+            kept = weigh_columns(q, factors, group, False)
+            pieces = split_sums(kept, got[n], len(group))
+            final += [
+                piece if s == 0 else swap(piece, "ka", s)
+                for piece, s in zip(pieces, group)
+            ]
+        return own_row(factors), final_sum(final[::-1])
+    factors, _ = solve_and_weigh(q, inv, tails, [0])
     whole = jnp.einsum("irj,ri->rj", q, factors, precision=HIGHEST)
     reduced = lax.psum_scatter(whole, ("ia", "ka"), scatter_dimension=1, tiled=True)
-    return a_row, reduced.reshape(rank, 1, reduced.shape[1])
+    return own_row(factors), reduced.reshape(rank, 1, reduced.shape[1])
+
+
+def chunks_of(n_ka):
+    return [[s] for s in reversed(range(2, n_ka))] + [[1, 0]]
 
 
 def solution(mesh):

time: 46.1 us -> 46 us (level)
  starting transfers between devices: 21.4 us -> 23.9 us
  waiting for transfers between devices: 10.9 us -> 8.86 us
  Pallas kernels: 12.9 us -> 12.4 us
    ppermute x17 -> x18, starting transfers between devices: 21.4 us -> 23.9 us  [swap(): return lax.ppermute(x, axis, [(i, i ^ s) for i in range(n)])]
    ppermute x17 -> x18, waiting for transfers between devices: 10.9 us -> 8.86 us  [swap(): return lax.ppermute(x, axis, [(i, i ^ s) for i in range(n)])]
    pallas_call x1, Pallas kernels: 6.35 us -> 5.09 us  [contract(): pl.pallas_call(functools.partial(contract_kernel, chunks=chunks), out_sha...]
    pallas_call x0 -> x1, Pallas kernels: none -> 0.68 us  [own_row(): pl.pallas_call(row_kernel, out_shape=jax.ShapeDtypeStruct((1, factors.sha...]
    pallas_call x3 -> x5, Pallas kernels: 1.09 us -> 1.6 us  [weigh_columns(): pl.pallas_call(functools.partial(weigh_kernel, shifts=shifts, other=other...]
  transfers between devices with their start and end apart: 17 -> 18, of which waited for: 6 -> 5; matrix products, arithmetic and copies ran while one was open for 0% -> 0% of each run, Pallas kernels for 23% -> 22%
where the time goes in v1:
time: 46 us; the launch traced here: 45.9 us
  starting transfers between devices  23.9 us (52%)
  Pallas kernels  12.4 us (27%)
  waiting for transfers between devices  8.86 us (19%)
  between operations  0.75 us (2%)
    ppermute x18, starting transfers between devices, swap(): return lax.ppermute(x, axis, [(i, i ^ s) for i in range(n)])  23.9 us
    ppermute x18, waiting for transfers between devices, swap(): return lax.ppermute(x, axis, [(i, i ^ s) for i in range(n)])  8.86 us
    pallas_call x1, Pallas kernels, contract(): pl.pallas_call(functools.partial(contract_kernel, chunks=chunks), out_sha...  5.09 us
    pallas_call x1, Pallas kernels, inverse(): pl.pallas_call(inverse_kernel, out_shape=pltpu.VMEM((rank, rank), F32), i...  2.13 us
    pallas_call x5, Pallas kernels, weigh_columns(): pl.pallas_call(functools.partial(weigh_kernel, shifts=shifts, other=other...  1.6 us
  transfers between devices with their start and end apart: 18, of which 5 were waited for; matrix products, arithmetic and copies ran while one was open for 0% of the time, Pallas kernels for 22%

profile of v1, /device:TPU:0, one launch (start us, length us, event | category | flops | bytes accessed | tf_op | source)
XLA Modules:
  0.0 45.9 jit_solution(448876476180279587)
XLA Ops:
  0.6 5.1 %collective-permute-start = (f32[64,512]{1,0:T(8,128)}, f32[64,512]{1,0:T(8,128)S(1)}, u32[]{:S(2)}, u32[]{:S(2)}) collective-permute-start(f32[64,512]{1,0:T(8,128)} %bitcast.1), channel_id=1, source_target_pairs={{0,3},{1,2},{2,1},{3,0},{4,7},{5,6},{6,5},{7,4},{8,11},{9,10},{10,... | collective-permute-start | bytes 393224 | tf_op jit(solution)/shard_map/ppermute | solution.py:450
  5.8 0.0 collective-permute-start.1
  5.8 0.6 %collective-permute-start.2 = (f32[64,512]{1,0:T(8,128)}, f32[64,512]{1,0:T(8,128)S(1)}, u32[]{:S(2)}, u32[]{:S(2)}) collective-permute-start(f32[64,512]{1,0:T(8,128)} %bitcast.3), channel_id=1, source_target_pairs={{0,1},{1,0},{2,3},{3,2},{4,5},{5,4},{6,7},{7,6},{8,9},{9,8},{10,11... | collective-permute-start | bytes 393224 | tf_op jit(solution)/shard_map/ppermute | solution.py:450
  6.4 5.1 %contract.1 = (f32[16,64,2048]{2,1,0:T(8,128)S(1)}, f32[32,128]{1,0:T(8,128)S(1)}, f32[32,128]{1,0:T(8,128)S(1)}) custom-call(f32[16,64,2048]{2,1,0:T(8,128)} %x_hbm.1, f32[64,512]{1,0:T(8,128)} %bitcast.4, f32[64,64]{1,0:T(8,128)} %c_hbm.1), custom_call_target="tpu_custom_call" | custom-call | flops 1073741824 | bytes 8388608 | tf_op jit(solution)/shard_map/contract/pallas_call | solution.py:91
  11.5 0.0 collective-permute-done.refs_1_
  11.5 0.9 %mode_one_early.1 = (f32[1024,128]{1,0:T(8,128)S(1)}, f32[32,128]{1,0:T(8,128)S(1)}) custom-call(f32[16,64,2048]{2,1,0:T(8,128)S(1)} %get-tuple-element.11.q_ref, f32[32,128]{1,0:T(8,128)S(1)} %get-tuple-element.12.own_ref, f32[64,512]{1,0:T(8,128)S(1)} %bitcast.5, f32[64,512]{1,0:T(8,128)S(1)} %collective-permute-done.refs_1_), custom_call_target="tpu_custom_call" | custom-call | flops 2097152 | bytes 4194304 | tf_op jit(solution)/shard_map/mode_one_early/pallas_call | solution.py:186
  12.4 4.7 %collective-permute-done.1.refs_0_ = f32[64,512]{1,0:T(8,128)S(1)} collective-permute-done((f32[64,512]{1,0:T(8,128)}, f32[64,512]{1,0:T(8,128)S(1)}, u32[]{:S(2)}, u32[]{:S(2)}) %collective-permute-start.1) | collective-permute-done | bytes 131104 | tf_op jit(solution)/shard_map/ppermute | solution.py:450
  17.1 0.0 collective-permute-done.2.refs_1_
  17.1 0.8 %mode_one_late.1.refs_0_ = f32[40,128]{1,0:T(8,128)S(1)} custom-call(f32[16,64,2048]{2,1,0:T(8,128)S(1)} %get-tuple-element.11.q_ref, f32[1024,128]{1,0:T(8,128)S(1)} %get-tuple-element.13.sums_ref, f32[32,128]{1,0:T(8,128)S(1)} %get-tuple-element.14.gram_ref, f32[64,512]{1,0:T(8,128)S(1)} %collective-permute-done.1.refs_0_, ...), custom_call_target="tpu_custom_call" | custom-call | flops 2097152 | bytes 4194304 | tf_op jit(solution)/shard_map/mode_one_late/pallas_call | solution.py:198
  17.9 0.1 collective-permute-start.3
  18.0 1.6 %collective-permute-start.4 = (f32[40,128]{1,0:T(8,128)S(1)}, f32[40,128]{1,0:T(8,128)S(1)}, u32[]{:S(2)}, u32[]{:S(2)}) collective-permute-start(f32[40,128]{1,0:T(8,128)S(1)} %mode_one_late.1.refs_0_), channel_id=1, source_target_pairs={{0,8},{4,12},{8,0},{12,4},{1,9},{5,13},{9,1},{13,5},{2,10},{6,14},... | collective-permute-start | bytes 61448 | tf_op jit(solution)/shard_map/ppermute | solution.py:450
  19.5 0.3 collective-permute-start.5
  19.8 0.0 collective-permute-start.6
  19.8 3.0 %collective-permute-start.7 = (f32[32,128]{1,0:T(8,128)S(1)}, f32[32,128]{1,0:T(8,128)S(1)}, u32[]{:S(2)}, u32[]{:S(2)}) collective-permute-start(f32[32,128]{1,0:T(8,128)S(1)} %get-tuple-element.15.refs_4_), channel_id=1, source_target_pairs={{0,2},{1,3},{2,0},{3,1},{4,6},{5,7},{6,4},{7,5},{8,10},{9,11},{10,... | collective-permute-start | bytes 49160 | tf_op jit(solution)/shard_map/ppermute | solution.py:450
  22.8 0.0 collective-permute-done.3.refs_1_
  22.8 1.3 %collective-permute-start.8 = (f32[32,128]{1,0:T(8,128)S(1)}, f32[32,128]{1,0:T(8,128)S(1)}, u32[]{:S(2)}, u32[]{:S(2)}) collective-permute-start(f32[32,128]{1,0:T(8,128)S(1)} %get-tuple-element.15.refs_4_), channel_id=1, source_target_pairs={{0,3},{1,2},{2,1},{3,0},{4,7},{5,6},{6,5},{7,4},{8,11},{9,10},{10,... | collective-permute-start | bytes 49160 | tf_op jit(solution)/shard_map/ppermute | solution.py:450
  24.2 0.0 collective-permute-done.4.refs_2_
  24.2 0.0 collective-permute-done.5.refs_3_
  24.2 0.2 collective-permute-start.10
  24.4 2.4 %collective-permute-start.11 = (f32[8,128]{1,0:T(8,128)S(1)}, f32[8,128]{1,0:T(8,128)S(1)}, u32[]{:S(2)}, u32[]{:S(2)}) collective-permute-start(f32[8,128]{1,0:T(8,128)S(1)} %add_tail.1.refs_0_), channel_id=1, source_target_pairs={{0,3},{1,2},{2,1},{3,0},{4,7},{5,6},{6,5},{7,4},{8,11},{9,10},{10,... | collective-permute-start | bytes 12296 | tf_op jit(solution)/shard_map/ppermute | solution.py:450
  26.8 0.0 collective-permute-done.6.refs_5_
  26.8 0.9 %collective-permute-start.9 = (f32[8,128]{1,0:T(8,128)S(1)}, f32[8,128]{1,0:T(8,128)S(1)}, u32[]{:S(2)}, u32[]{:S(2)}) collective-permute-start(f32[8,128]{1,0:T(8,128)S(1)} %add_tail.1.refs_0_), channel_id=1, source_target_pairs={{0,1},{1,0},{2,3},{3,2},{4,5},{5,4},{6,7},{7,6},{8,9},{9,8},{10,11... | collective-permute-start | bytes 12296 | tf_op jit(solution)/shard_map/ppermute | solution.py:450
  27.8 0.0 collective-permute-done.7.refs_6_
  27.8 0.7 %collective-permute-done.8.refs_7_ = f32[32,128]{1,0:T(8,128)S(1)} collective-permute-done((f32[32,128]{1,0:T(8,128)S(1)}, f32[32,128]{1,0:T(8,128)S(1)}, u32[]{:S(2)}, u32[]{:S(2)}) %collective-permute-start.8) | collective-permute-done | bytes 16416 | tf_op jit(solution)/shard_map/ppermute | solution.py:450
  28.4 2.1 %inverse.1.inv_ref = f32[64,64]{1,0:T(8,128)S(1)} custom-call(f32[40,128]{1,0:T(8,128)S(1)} %mode_one_late.1.refs_0_, f32[40,128]{1,0:T(8,128)S(1)} %collective-permute-done.3.refs_1_, f32[40,128]{1,0:T(8,128)S(1)} %collective-permute-done.4.refs_2_, f32[40,128]{1,0:T(8,128)S(1)} %collective-permute-done.5.refs_3_, f32[32,128]{1,0:T(8,128)S(1)} %get-tuple-element.15.refs_4_, ...), custom_call_target="tpu_custom_call" | custom-call | flops 4000000 | bytes 4000000 | tf_op jit(solution)/shard_map/inverse/pallas_call | solution.py:296
  30.6 0.0 collective-permute-done.10.refs_2_
  30.6 0.0 collective-permute-done.11.refs_3_
  30.6 0.0 collective-permute-done.9.refs_1_
  30.6 0.5 %solve.1 = (f32[64,16]{1,0:T(8,128)S(1)}, f32[64,256]{1,0:T(8,128)S(1)}) custom-call(f32[16,64,2048]{2,1,0:T(8,128)S(1)} %get-tuple-element.11.q_ref, f32[64,64]{1,0:T(8,128)S(1)} %inverse.1.inv_ref, f32[8,128]{1,0:T(8,128)S(1)} %add_tail.1.refs_0_, f32[8,128]{1,0:T(8,128)S(1)} %collective-permute-done.9.refs_1_, ...), custom_call_target="tpu_custom_call" | custom-call | flops 524288 | bytes 1048576 | tf_op jit(solution)/shard_map/solve/pallas_call | solution.py:388
  31.1 0.4 weigh.6
  31.5 1.6 %collective-permute-start.12 = (f32[64,512]{1,0:T(8,128)S(1)}, f32[64,512]{1,0:T(8,128)S(1)}, u32[]{:S(2)}, u32[]{:S(2)}) collective-permute-start(f32[64,512]{1,0:T(8,128)S(1)} %weigh.6), channel_id=1, source_target_pairs={{0,16},{16,0},{1,17},{17,1},{2,18},{18,2},{3,19},{19,3},{4,20},{20... | collective-permute-start | bytes 393224 | tf_op jit(solution)/shard_map/ppermute | solution.py:450
  33.0 0.5 %collective-permute-start.16 = (f32[64,256]{1,0:T(8,128)S(1)}, f32[64,256]{1,0:T(8,128)S(1)}, u32[]{:S(2)}, u32[]{:S(2)}) collective-permute-start(f32[64,256]{1,0:T(8,128)S(1)} %get-tuple-element.19), channel_id=1, source_target_pairs={{0,16},{16,0},{1,17},{17,1},{2,18},{18,2},{3,19},{19,3},{4,20},{20... | collective-permute-start | bytes 196616 | tf_op jit(solution)/shard_map/ppermute | solution.py:450
  33.6 0.3 weigh.8
  33.8 1.6 %collective-permute-start.14 = (f32[64,256]{1,0:T(8,128)S(1)}, f32[64,256]{1,0:T(8,128)S(1)}, u32[]{:S(2)}, u32[]{:S(2)}) collective-permute-start(f32[64,256]{1,0:T(8,128)S(1)} %weigh.8), channel_id=1, source_target_pairs={{0,16},{16,0},{1,17},{17,1},{2,18},{18,2},{3,19},{19,3},{4,20},{20... | collective-permute-start | bytes 196616 | tf_op jit(solution)/shard_map/ppermute | solution.py:450
  35.4 0.3 weigh.9.kept_ref
  35.7 0.3 weigh.7.kept_ref
  36.0 0.4 weigh.5.kept_ref
  36.4 1.2 %collective-permute-done.16.got_ref = f32[64,256]{1,0:T(8,128)S(1)} collective-permute-done((f32[64,256]{1,0:T(8,128)S(1)}, f32[64,256]{1,0:T(8,128)S(1)}, u32[]{:S(2)}, u32[]{:S(2)}) %collective-permute-start.16) | collective-permute-done | bytes 65568 | tf_op jit(solution)/shard_map/ppermute | solution.py:450
  37.7 2.0 %collective-permute-start.17 = (f32[64,256]{1,0:T(8,128)S(1)}, f32[64,256]{1,0:T(8,128)S(1)}, u32[]{:S(2)}, u32[]{:S(2)}) collective-permute-start(f32[64,256]{1,0:T(8,128)S(1)} %split_sums.5), channel_id=1, source_target_pairs={{0,3},{1,2},{2,1},{3,0},{4,7},{5,6},{6,5},{7,4},{8,11},{9,10},{10,... | collective-permute-start | bytes 196616 | tf_op jit(solution)/shard_map/ppermute | solution.py:450
  39.6 0.0 collective-permute-done.14.got_ref
  39.6 0.4 collective-permute-start.15
  40.1 0.0 collective-permute-done.12.got_ref
  40.1 2.2 %collective-permute-start.13 = (f32[64,256]{1,0:T(8,128)S(1)}, f32[64,256]{1,0:T(8,128)S(1)}, u32[]{:S(2)}, u32[]{:S(2)}) collective-permute-start(f32[64,256]{1,0:T(8,128)S(1)} %get-tuple-element.18), channel_id=1, source_target_pairs={{0,1},{1,0},{2,3},{3,2},{4,5},{5,4},{6,7},{7,6},{8,9},{9,8},{10,11... | collective-permute-start | bytes 196616 | tf_op jit(solution)/shard_map/ppermute | solution.py:450
  42.3 0.7 %own_row.1 = f32[1,64]{1,0:T(1,128)} custom-call(f32[64,16]{1,0:T(8,128)S(1)} %get-tuple-element.16.factors_ref), custom_call_target="tpu_custom_call" | custom-call | tf_op jit(solution)/shard_map/own_row/pallas_call | solution.py:362
  43.0 0.8 %collective-permute-done.17.refs_3_ = f32[64,256]{1,0:T(8,128)S(1)} collective-permute-done((f32[64,256]{1,0:T(8,128)S(1)}, f32[64,256]{1,0:T(8,128)S(1)}, u32[]{:S(2)}, u32[]{:S(2)}) %collective-permute-start.17) | collective-permute-done | bytes 65568 | tf_op jit(solution)/shard_map/ppermute | solution.py:450
  43.8 1.4 %collective-permute-done.15.refs_2_ = f32[64,256]{1,0:T(8,128)S(1)} collective-permute-done((f32[64,256]{1,0:T(8,128)S(1)}, f32[64,256]{1,0:T(8,128)S(1)}, u32[]{:S(2)}, u32[]{:S(2)}) %collective-permute-start.15) | collective-permute-done | bytes 65568 | tf_op jit(solution)/shard_map/ppermute | solution.py:450
  45.2 0.0 collective-permute-done.13.refs_1_
  45.2 0.7 %final_sum.1 = f32[64,1,256]{2,1,0:T(1,128)} custom-call(f32[64,256]{1,0:T(8,128)S(1)} %get-tuple-element.17.refs_0_, f32[64,256]{1,0:T(8,128)S(1)} %collective-permute-done.13.refs_1_, f32[64,256]{1,0:T(8,128)S(1)} %collective-permute-done.15.refs_2_, f32[64,256]{1,0:T(8,128)S(1)} %collective-permute-done.17.refs_3_), custom_call_target="tpu_custom_call" | custom-call | tf_op jit(solution)/shard_map/final_sum/pallas_call | solution.py:438
  (6 shorter events, 0.0 us)
Async XLA Ops:
  0.6 10.9 %copy-start = (f32[512,64]{0,1:T(8,128)S(1)}, f32[512,64]{0,1:T(8,128)}, u32[]{:S(2)}) copy-start(f32[512,64]{0,1:T(8,128)} %param.4) | copy-start | bytes 393220
  0.6 10.9 %collective-permute-start = (f32[64,512]{1,0:T(8,128)}, f32[64,512]{1,0:T(8,128)S(1)}, u32[]{:S(2)}, u32[]{:S(2)}) collective-permute-start(f32[64,512]{1,0:T(8,128)} %bitcast.1), channel_id=1, source_target_pairs={{0,3},{1,2},{2,1},{3,0},{4,7},{5,6},{6,5},{7,4},{8,11},{9,10},{10,... | collective-permute-start | bytes 393224 | tf_op jit(solution)/shard_map/ppermute | solution.py:450
  5.8 11.3 %collective-permute-start.1 = (f32[64,512]{1,0:T(8,128)}, f32[64,512]{1,0:T(8,128)S(1)}, u32[]{:S(2)}, u32[]{:S(2)}) collective-permute-start(f32[64,512]{1,0:T(8,128)} %bitcast.2), channel_id=1, source_target_pairs={{0,2},{1,3},{2,0},{3,1},{4,6},{5,7},{6,4},{7,5},{8,10},{9,11},{10,... | collective-permute-start | bytes 393224 | tf_op jit(solution)/shard_map/ppermute | solution.py:450
  5.8 11.3 %collective-permute-start.2 = (f32[64,512]{1,0:T(8,128)}, f32[64,512]{1,0:T(8,128)S(1)}, u32[]{:S(2)}, u32[]{:S(2)}) collective-permute-start(f32[64,512]{1,0:T(8,128)} %bitcast.3), channel_id=1, source_target_pairs={{0,1},{1,0},{2,3},{3,2},{4,5},{5,4},{6,7},{7,6},{8,9},{9,8},{10,11... | collective-permute-start | bytes 393224 | tf_op jit(solution)/shard_map/ppermute | solution.py:450
  17.9 5.0 %collective-permute-start.3 = (f32[40,128]{1,0:T(8,128)S(1)}, f32[40,128]{1,0:T(8,128)S(1)}, u32[]{:S(2)}, u32[]{:S(2)}) collective-permute-start(f32[40,128]{1,0:T(8,128)S(1)} %mode_one_late.1.refs_0_), channel_id=1, source_target_pairs={{0,4},{4,0},{8,12},{12,8},{1,5},{5,1},{9,13},{13,9},{2,6},{6,2},{1... | collective-permute-start | bytes 61448 | tf_op jit(solution)/shard_map/ppermute | solution.py:450
  18.0 6.2 %collective-permute-start.4 = (f32[40,128]{1,0:T(8,128)S(1)}, f32[40,128]{1,0:T(8,128)S(1)}, u32[]{:S(2)}, u32[]{:S(2)}) collective-permute-start(f32[40,128]{1,0:T(8,128)S(1)} %mode_one_late.1.refs_0_), channel_id=1, source_target_pairs={{0,8},{4,12},{8,0},{12,4},{1,9},{5,13},{9,1},{13,5},{2,10},{6,14},... | collective-permute-start | bytes 61448 | tf_op jit(solution)/shard_map/ppermute | solution.py:450
  19.5 4.7 %collective-permute-start.5 = (f32[40,128]{1,0:T(8,128)S(1)}, f32[40,128]{1,0:T(8,128)S(1)}, u32[]{:S(2)}, u32[]{:S(2)}) collective-permute-start(f32[40,128]{1,0:T(8,128)S(1)} %mode_one_late.1.refs_0_), channel_id=1, source_target_pairs={{0,12},{4,8},{8,4},{12,0},{1,13},{5,9},{9,5},{13,1},{2,14},{6,10},... | collective-permute-start | bytes 61448 | tf_op jit(solution)/shard_map/ppermute | solution.py:450
  19.8 7.0 %collective-permute-start.6 = (f32[32,128]{1,0:T(8,128)S(1)}, f32[32,128]{1,0:T(8,128)S(1)}, u32[]{:S(2)}, u32[]{:S(2)}) collective-permute-start(f32[32,128]{1,0:T(8,128)S(1)} %get-tuple-element.15.refs_4_), channel_id=1, source_target_pairs={{0,1},{1,0},{2,3},{3,2},{4,5},{5,4},{6,7},{7,6},{8,9},{9,8},{10,11... | collective-permute-start | bytes 49160 | tf_op jit(solution)/shard_map/ppermute | solution.py:450
  19.8 8.0 %collective-permute-start.7 = (f32[32,128]{1,0:T(8,128)S(1)}, f32[32,128]{1,0:T(8,128)S(1)}, u32[]{:S(2)}, u32[]{:S(2)}) collective-permute-start(f32[32,128]{1,0:T(8,128)S(1)} %get-tuple-element.15.refs_4_), channel_id=1, source_target_pairs={{0,2},{1,3},{2,0},{3,1},{4,6},{5,7},{6,4},{7,5},{8,10},{9,11},{10,... | collective-permute-start | bytes 49160 | tf_op jit(solution)/shard_map/ppermute | solution.py:450
  22.8 5.6 %collective-permute-start.8 = (f32[32,128]{1,0:T(8,128)S(1)}, f32[32,128]{1,0:T(8,128)S(1)}, u32[]{:S(2)}, u32[]{:S(2)}) collective-permute-start(f32[32,128]{1,0:T(8,128)S(1)} %get-tuple-element.15.refs_4_), channel_id=1, source_target_pairs={{0,3},{1,2},{2,1},{3,0},{4,7},{5,6},{6,5},{7,4},{8,11},{9,10},{10,... | collective-permute-start | bytes 49160 | tf_op jit(solution)/shard_map/ppermute | solution.py:450
  24.2 6.3 %collective-permute-start.10 = (f32[8,128]{1,0:T(8,128)S(1)}, f32[8,128]{1,0:T(8,128)S(1)}, u32[]{:S(2)}, u32[]{:S(2)}) collective-permute-start(f32[8,128]{1,0:T(8,128)S(1)} %add_tail.1.refs_0_), channel_id=1, source_target_pairs={{0,2},{1,3},{2,0},{3,1},{4,6},{5,7},{6,4},{7,5},{8,10},{9,11},{10,... | collective-permute-start | bytes 12296 | tf_op jit(solution)/shard_map/ppermute | solution.py:450
  24.4 6.2 %collective-permute-start.11 = (f32[8,128]{1,0:T(8,128)S(1)}, f32[8,128]{1,0:T(8,128)S(1)}, u32[]{:S(2)}, u32[]{:S(2)}) collective-permute-start(f32[8,128]{1,0:T(8,128)S(1)} %add_tail.1.refs_0_), channel_id=1, source_target_pairs={{0,3},{1,2},{2,1},{3,0},{4,7},{5,6},{6,5},{7,4},{8,11},{9,10},{10,... | collective-permute-start | bytes 12296 | tf_op jit(solution)/shard_map/ppermute | solution.py:450
  26.8 3.7 %collective-permute-start.9 = (f32[8,128]{1,0:T(8,128)S(1)}, f32[8,128]{1,0:T(8,128)S(1)}, u32[]{:S(2)}, u32[]{:S(2)}) collective-permute-start(f32[8,128]{1,0:T(8,128)S(1)} %add_tail.1.refs_0_), channel_id=1, source_target_pairs={{0,1},{1,0},{2,3},{3,2},{4,5},{5,4},{6,7},{7,6},{8,9},{9,8},{10,11... | collective-permute-start | bytes 12296 | tf_op jit(solution)/shard_map/ppermute | solution.py:450
  31.5 8.6 %collective-permute-start.12 = (f32[64,512]{1,0:T(8,128)S(1)}, f32[64,512]{1,0:T(8,128)S(1)}, u32[]{:S(2)}, u32[]{:S(2)}) collective-permute-start(f32[64,512]{1,0:T(8,128)S(1)} %weigh.6), channel_id=1, source_target_pairs={{0,16},{16,0},{1,17},{17,1},{2,18},{18,2},{3,19},{19,3},{4,20},{20... | collective-permute-start | bytes 393224 | tf_op jit(solution)/shard_map/ppermute | solution.py:450
  33.0 4.6 %collective-permute-start.16 = (f32[64,256]{1,0:T(8,128)S(1)}, f32[64,256]{1,0:T(8,128)S(1)}, u32[]{:S(2)}, u32[]{:S(2)}) collective-permute-start(f32[64,256]{1,0:T(8,128)S(1)} %get-tuple-element.19), channel_id=1, source_target_pairs={{0,16},{16,0},{1,17},{17,1},{2,18},{18,2},{3,19},{19,3},{4,20},{20... | collective-permute-start | bytes 196616 | tf_op jit(solution)/shard_map/ppermute | solution.py:450
  33.8 5.8 %collective-permute-start.14 = (f32[64,256]{1,0:T(8,128)S(1)}, f32[64,256]{1,0:T(8,128)S(1)}, u32[]{:S(2)}, u32[]{:S(2)}) collective-permute-start(f32[64,256]{1,0:T(8,128)S(1)} %weigh.8), channel_id=1, source_target_pairs={{0,16},{16,0},{1,17},{17,1},{2,18},{18,2},{3,19},{19,3},{4,20},{20... | collective-permute-start | bytes 196616 | tf_op jit(solution)/shard_map/ppermute | solution.py:450
  37.7 6.1 %collective-permute-start.17 = (f32[64,256]{1,0:T(8,128)S(1)}, f32[64,256]{1,0:T(8,128)S(1)}, u32[]{:S(2)}, u32[]{:S(2)}) collective-permute-start(f32[64,256]{1,0:T(8,128)S(1)} %split_sums.5), channel_id=1, source_target_pairs={{0,3},{1,2},{2,1},{3,0},{4,7},{5,6},{6,5},{7,4},{8,11},{9,10},{10,... | collective-permute-start | bytes 196616 | tf_op jit(solution)/shard_map/ppermute | solution.py:450
  39.6 5.6 %collective-permute-start.15 = (f32[64,256]{1,0:T(8,128)S(1)}, f32[64,256]{1,0:T(8,128)S(1)}, u32[]{:S(2)}, u32[]{:S(2)}) collective-permute-start(f32[64,256]{1,0:T(8,128)S(1)} %split_sums.4), channel_id=1, source_target_pairs={{0,2},{1,3},{2,0},{3,1},{4,6},{5,7},{6,4},{7,5},{8,10},{9,11},{10,... | collective-permute-start | bytes 196616 | tf_op jit(solution)/shard_map/ppermute | solution.py:450
  40.1 5.1 %collective-permute-start.13 = (f32[64,256]{1,0:T(8,128)S(1)}, f32[64,256]{1,0:T(8,128)S(1)}, u32[]{:S(2)}, u32[]{:S(2)}) collective-permute-start(f32[64,256]{1,0:T(8,128)S(1)} %get-tuple-element.18), channel_id=1, source_target_pairs={{0,1},{1,0},{2,3},{3,2},{4,5},{5,4},{6,7},{7,6},{8,9},{9,8},{10,11... | collective-permute-start | bytes 196616 | tf_op jit(solution)/shard_map/ppermute | solution.py:450

commit v2 on v1

--- a/solution.py
+++ b/solution.py
@@ -177,7 +177,7 @@
     row_block, rank, width = q.shape
     lines = row_block * rank // LANES
     count = len(parts)
-    split = {0, count - 1}
+    split = set(range(count)) - {count - 1}
     early = [s for s in range(count) if s in split]
     late = [s for s in reversed(range(count)) if s not in split]
     params = pltpu.CompilerParams(vmem_limit_bytes=6 << 20)
@@ -304,16 +304,11 @@
     )(*grams_b, *grams_c)
 
 
-def weigh(q_ref, factors, outs):
+def weigh(q_ref, weight_of, outs):
     row_block, rank, _ = q_ref.shape
     for tile in range(rank // SUBLANES):
         rows = pl.ds(tile * SUBLANES, SUBLANES)
-        weights = [
-            jnp.broadcast_to(
-                factors[tile * SUBLANES : (tile + 1) * SUBLANES, i : i + 1], (SUBLANES, LANES)
-            )
-            for i in range(row_block)
-        ]
+        weights = [weight_of(tile, i) for i in range(row_block)]
         for out_ref, start, at, width in outs:
             for c in range(0, width, LANES):
                 columns = pl.ds(pl.multiple_of(start + c, LANES), LANES)
@@ -321,6 +316,11 @@
                 for i in range(1, row_block):
                     total = total + weights[i] * q_ref[i, rows, columns]
                 out_ref[rows, at + c : at + c + LANES] = total
+
+
+def weight_rows(tile, i, row_block):
+    at = (tile * row_block + i) * SUBLANES
+    return slice(at, at + SUBLANES)
 
 
 def targets(q_ref, out_ref, shifts, other):
@@ -336,7 +336,7 @@
 
 
 def solve_kernel(q_ref, inv_ref, *refs, shifts):
-    sum_refs, (factors_ref, send_ref) = refs[:-2], refs[-2:]
+    sum_refs, (factors_ref, weights_ref, send_ref) = refs[:-3], refs[-3:]
     row_block, rank, _ = q_ref.shape
     packed = total_of(sum_refs)
     columns = []
@@ -347,7 +347,14 @@
         )
     factors = dot(inv_ref[...], jnp.concatenate(columns, axis=0), NN)
     factors_ref[...] = factors
-    weigh(q_ref, factors, targets(q_ref, send_ref, shifts, True))
+
+    def weight_of(tile, i):
+        rows = slice(tile * SUBLANES, (tile + 1) * SUBLANES)
+        weight = jnp.broadcast_to(factors[rows, i : i + 1], (SUBLANES, LANES))
+        weights_ref[weight_rows(tile, i, row_block), :] = weight
+        return weight
+
+    weigh(q_ref, weight_of, targets(q_ref, send_ref, shifts, True))
 
 
 def row_kernel(factors_ref, out_ref):
@@ -369,8 +376,11 @@
     )(factors)
 
 
-def weigh_kernel(q_ref, factors_ref, out_ref, *, shifts, other):
-    weigh(q_ref, factors_ref[...], targets(q_ref, out_ref, shifts, other))
+def weigh_kernel(q_ref, weights_ref, out_ref, *, shifts, other):
+    def weight_of(tile, i):
+        return weights_ref[weight_rows(tile, i, q_ref.shape[0]), :]
+
+    weigh(q_ref, weight_of, targets(q_ref, out_ref, shifts, other))
 
 
 def share(q, shifts):
@@ -387,16 +397,20 @@
     shape, work = share(q, shifts)
     return pl.pallas_call(
         functools.partial(solve_kernel, shifts=shifts),
-        out_shape=(pltpu.VMEM((rank, row_block), F32), shape),
+        out_shape=(
+            pltpu.VMEM((rank, row_block), F32),
+            pltpu.VMEM((rank * row_block, LANES), F32),
+            shape,
+        ),
         in_specs=[VMEM] * (2 + len(sums)),
-        out_specs=[VMEM] * 2,
+        out_specs=[VMEM] * 3,
         compiler_params=pltpu.CompilerParams(vmem_limit_bytes=4 << 20),
         cost_estimate=work,
         name="solve",
     )(placed_in(q, pltpu.VMEM), inv, *sums)
 
 
-def weigh_columns(q, factors, shifts, other):
+def weigh_columns(q, weights, shifts, other):
     shape, work = share(q, shifts)
     return pl.pallas_call(
         functools.partial(weigh_kernel, shifts=shifts, other=other),
@@ -406,7 +420,7 @@
         compiler_params=pltpu.CompilerParams(vmem_limit_bytes=4 << 20),
         cost_estimate=work,
         name="weigh",
-    )(placed_in(q, pltpu.VMEM), factors)
+    )(placed_in(q, pltpu.VMEM), weights)
 
 
 def split_kernel(kept_ref, got_ref, *out_refs):
@@ -453,6 +467,15 @@
 def swaps(x, axis):
     n = lax.axis_size(axis)
     return [x] + [swap(x, axis, s) for s in range(1, n)]
+
+
+def crossed(x):
+    n_ja, n_ka = lax.axis_size("ja"), lax.axis_size("ka")
+    got = [x]
+    for s in range(1, n_ka):
+        pairs = [(i, i ^ (n_ka + s)) for i in range(n_ja * n_ka)]
+        got.append(lax.ppermute(x, ("ja", "ka"), pairs))
+    return got
 
 
 def body(tensor, factor_b, factor_c):
@@ -465,25 +488,25 @@
     q, own_gram, gram_c = contract(tensor, bt, factor_c)
     grams_c = swaps(gram_c, "ka")
     sums = swaps(mode_one_sums(q, own_gram, parts), "ja")
-    tails = swaps(add_tail(sums, lines), "ka")
+    tails = crossed(add_tail(sums, lines))
     inv = inverse(sums, grams_c)
     if n_ia == 2 and width % (n_ia * n_ka * LANES) == 0:
         groups = chunks_of(n_ka)
-        factors, sent = solve_and_weigh(q, inv, tails, groups[0])
+        factors, weights, sent = solve_and_weigh(q, inv, tails, groups[0])
         got = [swap(sent, "ia", 1)]
         for n, group in enumerate(groups[1:], 1):
-            sent = weigh_columns(q, factors, group, True)
+            sent = weigh_columns(q, weights, group, True)
             got.append(swap(sent, "ia", 1))
         final = []
         for n, group in enumerate(groups):
-            kept = weigh_columns(q, factors, group, False)
+            kept = weigh_columns(q, weights, group, False)
             pieces = split_sums(kept, got[n], len(group))
             final += [
                 piece if s == 0 else swap(piece, "ka", s)
                 for piece, s in zip(pieces, group)
             ]
         return own_row(factors), final_sum(final[::-1])
-    factors, _ = solve_and_weigh(q, inv, tails, [0])
+    factors, _, _ = solve_and_weigh(q, inv, tails, [0])
     whole = jnp.einsum("irj,ri->rj", q, factors, precision=HIGHEST)
     reduced = lax.psum_scatter(whole, ("ia", "ka"), scatter_dimension=1, tiled=True)
     return own_row(factors), reduced.reshape(rank, 1, reduced.shape[1])

time: 46 us -> 48 us (1.043)
  waiting for transfers between devices: 8.86 us -> 12.3 us
  starting transfers between devices: 23.9 us -> 22.9 us
  Pallas kernels: 12.4 us -> 11.9 us
    ppermute x18 -> x15, starting transfers between devices: 23.9 us -> 20.3 us  [swap(): return lax.ppermute(x, axis, [(i, i ^ s) for i in range(n)])]
    ppermute x18 -> x15, waiting for transfers between devices: 8.86 us -> 12.3 us  [swap(): return lax.ppermute(x, axis, [(i, i ^ s) for i in range(n)])]
    ppermute x0 -> x3, starting transfers between devices: none -> 2.63 us  [crossed(): got.append(lax.ppermute(x, ('ja', 'ka'), pairs))]
  transfers between devices with their start and end apart: 18 -> 18, of which waited for: 5 -> 5; matrix products, arithmetic and copies ran while one was open for 0% -> 0% of each run, Pallas kernels for 22% -> 21%
where the time goes in v2:
time: 48 us; the launch traced here: 47.9 us
  starting transfers between devices  22.9 us (48%)
  waiting for transfers between devices  12.3 us (26%)
  Pallas kernels  11.9 us (25%)
  between operations  0.73 us (2%)
    ppermute x15, starting transfers between devices, swap(): return lax.ppermute(x, axis, [(i, i ^ s) for i in range(n)])  20.3 us
    ppermute x15, waiting for transfers between devices, swap(): return lax.ppermute(x, axis, [(i, i ^ s) for i in range(n)])  12.3 us
    pallas_call x1, Pallas kernels, contract(): pl.pallas_call(functools.partial(contract_kernel, chunks=chunks), out_sha...  5.09 us
    ppermute x3, starting transfers between devices, crossed(): got.append(lax.ppermute(x, ('ja', 'ka'), pairs))  2.63 us
    pallas_call x1, Pallas kernels, inverse(): pl.pallas_call(inverse_kernel, out_shape=pltpu.VMEM((rank, rank), F32), i...  2.13 us
    pallas_call x1, Pallas kernels, mode_one_sums(): pl.pallas_call(functools.partial(early_kernel, shifts=early), out_shape=(...  1.19 us
    pallas_call x5, Pallas kernels, weigh_columns(): pl.pallas_call(functools.partial(weigh_kernel, shifts=shifts, other=other...  1.14 us
  transfers between devices with their start and end apart: 18, of which 5 were waited for; matrix products, arithmetic and copies ran while one was open for 0% of the time, Pallas kernels for 21%

profile of v2, /device:TPU:0, one launch (start us, length us, event | category | flops | bytes accessed | tf_op | source)
XLA Modules:
  0.0 47.9 jit_solution(15031988795161809491)
XLA Ops:
  0.6 3.1 %collective-permute-start = (f32[64,512]{1,0:T(8,128)}, f32[64,512]{1,0:T(8,128)S(1)}, u32[]{:S(2)}, u32[]{:S(2)}) collective-permute-start(f32[64,512]{1,0:T(8,128)} %bitcast.1), channel_id=1, source_target_pairs={{0,1},{1,0},{2,3},{3,2},{4,5},{5,4},{6,7},{7,6},{8,9},{9,8},{10,11... | collective-permute-start | bytes 393224 | tf_op jit(solution)/shard_map/ppermute | solution.py:464
  3.8 2.6 %collective-permute-start.1 = (f32[64,512]{1,0:T(8,128)}, f32[64,512]{1,0:T(8,128)S(1)}, u32[]{:S(2)}, u32[]{:S(2)}) collective-permute-start(f32[64,512]{1,0:T(8,128)} %bitcast.2), channel_id=1, source_target_pairs={{0,2},{1,3},{2,0},{3,1},{4,6},{5,7},{6,4},{7,5},{8,10},{9,11},{10,... | collective-permute-start | bytes 393224 | tf_op jit(solution)/shard_map/ppermute | solution.py:464
  6.3 0.0 collective-permute-start.2
  6.3 5.1 %contract.1 = (f32[16,64,2048]{2,1,0:T(8,128)S(1)}, f32[32,128]{1,0:T(8,128)S(1)}, f32[32,128]{1,0:T(8,128)S(1)}) custom-call(f32[16,64,2048]{2,1,0:T(8,128)} %x_hbm.1, f32[64,512]{1,0:T(8,128)} %bitcast.4, f32[64,64]{1,0:T(8,128)} %c_hbm.1), custom_call_target="tpu_custom_call" | custom-call | flops 1073741824 | bytes 8388608 | tf_op jit(solution)/shard_map/contract/pallas_call | solution.py:91
  11.4 0.0 collective-permute-done.refs_1_
  11.5 5.4 %collective-permute-done.1.refs_2_ = f32[64,512]{1,0:T(8,128)S(1)} collective-permute-done((f32[64,512]{1,0:T(8,128)}, f32[64,512]{1,0:T(8,128)S(1)}, u32[]{:S(2)}, u32[]{:S(2)}) %collective-permute-start.1) | collective-permute-done | bytes 131104 | tf_op jit(solution)/shard_map/ppermute | solution.py:464
  16.9 1.2 %mode_one_early.1 = (f32[1024,128]{1,0:T(8,128)S(1)}, f32[32,128]{1,0:T(8,128)S(1)}) custom-call(f32[16,64,2048]{2,1,0:T(8,128)S(1)} %get-tuple-element.12.q_ref, f32[32,128]{1,0:T(8,128)S(1)} %get-tuple-element.13.own_ref, f32[64,512]{1,0:T(8,128)S(1)} %bitcast.5, f32[64,512]{1,0:T(8,128)S(1)} %collective-permute-done.refs_1_, ...), custom_call_target="tpu_custom_call" | custom-call | flops 2097152 | bytes 4194304 | tf_op jit(solution)/shard_map/mode_one_early/pallas_call | solution.py:186
  18.1 0.0 collective-permute-done.2.refs_0_
  18.1 0.5 %mode_one_late.1.refs_0_ = f32[40,128]{1,0:T(8,128)S(1)} custom-call(f32[16,64,2048]{2,1,0:T(8,128)S(1)} %get-tuple-element.12.q_ref, f32[1024,128]{1,0:T(8,128)S(1)} %get-tuple-element.14.sums_ref, f32[32,128]{1,0:T(8,128)S(1)} %get-tuple-element.15.gram_ref, f32[64,512]{1,0:T(8,128)S(1)} %collective-permute-done.2.refs_0_), custom_call_target="tpu_custom_call" | custom-call | flops 2097152 | bytes 4194304 | tf_op jit(solution)/shard_map/mode_one_late/pallas_call | solution.py:198
  18.6 0.1 collective-permute-start.3
  18.7 1.6 %collective-permute-start.4 = (f32[40,128]{1,0:T(8,128)S(1)}, f32[40,128]{1,0:T(8,128)S(1)}, u32[]{:S(2)}, u32[]{:S(2)}) collective-permute-start(f32[40,128]{1,0:T(8,128)S(1)} %mode_one_late.1.refs_0_), channel_id=1, source_target_pairs={{0,8},{4,12},{8,0},{12,4},{1,9},{5,13},{9,1},{13,5},{2,10},{6,14},... | collective-permute-start | bytes 61448 | tf_op jit(solution)/shard_map/ppermute | solution.py:464
  20.2 0.3 collective-permute-start.5
  20.5 0.8 %collective-permute-start.6 = (f32[32,128]{1,0:T(8,128)S(1)}, f32[32,128]{1,0:T(8,128)S(1)}, u32[]{:S(2)}, u32[]{:S(2)}) collective-permute-start(f32[32,128]{1,0:T(8,128)S(1)} %get-tuple-element.16.refs_4_), channel_id=1, source_target_pairs={{0,1},{1,0},{2,3},{3,2},{4,5},{5,4},{6,7},{7,6},{8,9},{9,8},{10,11... | collective-permute-start | bytes 49160 | tf_op jit(solution)/shard_map/ppermute | solution.py:464
  21.3 2.0 %collective-permute-start.7 = (f32[32,128]{1,0:T(8,128)S(1)}, f32[32,128]{1,0:T(8,128)S(1)}, u32[]{:S(2)}, u32[]{:S(2)}) collective-permute-start(f32[32,128]{1,0:T(8,128)S(1)} %get-tuple-element.16.refs_4_), channel_id=1, source_target_pairs={{0,2},{1,3},{2,0},{3,1},{4,6},{5,7},{6,4},{7,5},{8,10},{9,11},{10,... | collective-permute-start | bytes 49160 | tf_op jit(solution)/shard_map/ppermute | solution.py:464
  23.3 0.0 collective-permute-done.3.refs_1_
  23.3 1.5 %collective-permute-start.8 = (f32[32,128]{1,0:T(8,128)S(1)}, f32[32,128]{1,0:T(8,128)S(1)}, u32[]{:S(2)}, u32[]{:S(2)}) collective-permute-start(f32[32,128]{1,0:T(8,128)S(1)} %get-tuple-element.16.refs_4_), channel_id=1, source_target_pairs={{0,3},{1,2},{2,1},{3,0},{4,7},{5,6},{6,5},{7,4},{8,11},{9,10},{10,... | collective-permute-start | bytes 49160 | tf_op jit(solution)/shard_map/ppermute | solution.py:464
  24.9 0.0 collective-permute-done.4.refs_2_
  24.9 0.0 collective-permute-done.5.refs_3_
  24.9 0.1 collective-permute-start.10
  25.0 2.0 %collective-permute-start.11 = (f32[8,128]{1,0:T(8,128)S(1)}, f32[8,128]{1,0:T(8,128)S(1)}, u32[]{:S(2)}, u32[]{:S(2)}) collective-permute-start(f32[8,128]{1,0:T(8,128)S(1)} %add_tail.1.refs_0_), channel_id=1, source_target_pairs={{0,7},{1,6},{2,5},{3,4},{4,3},{5,2},{6,1},{7,0},{8,15},{9,14},{10,... | collective-permute-start | bytes 12296 | tf_op jit(solution)/shard_map/ppermute | solution.py:477
  27.0 0.0 collective-permute-done.6.refs_5_
  27.0 0.6 %collective-permute-start.9 = (f32[8,128]{1,0:T(8,128)S(1)}, f32[8,128]{1,0:T(8,128)S(1)}, u32[]{:S(2)}, u32[]{:S(2)}) collective-permute-start(f32[8,128]{1,0:T(8,128)S(1)} %add_tail.1.refs_0_), channel_id=1, source_target_pairs={{0,5},{1,4},{2,7},{3,6},{4,1},{5,0},{6,3},{7,2},{8,13},{9,12},{10,... | collective-permute-start | bytes 12296 | tf_op jit(solution)/shard_map/ppermute | solution.py:477
  27.5 0.0 collective-permute-done.7.refs_6_
  27.5 1.3 %collective-permute-done.8.refs_7_ = f32[32,128]{1,0:T(8,128)S(1)} collective-permute-done((f32[32,128]{1,0:T(8,128)S(1)}, f32[32,128]{1,0:T(8,128)S(1)}, u32[]{:S(2)}, u32[]{:S(2)}) %collective-permute-start.8) | collective-permute-done | bytes 16416 | tf_op jit(solution)/shard_map/ppermute | solution.py:464
  28.9 2.1 %inverse.1.inv_ref = f32[64,64]{1,0:T(8,128)S(1)} custom-call(f32[40,128]{1,0:T(8,128)S(1)} %mode_one_late.1.refs_0_, f32[40,128]{1,0:T(8,128)S(1)} %collective-permute-done.3.refs_1_, f32[40,128]{1,0:T(8,128)S(1)} %collective-permute-done.4.refs_2_, f32[40,128]{1,0:T(8,128)S(1)} %collective-permute-done.5.refs_3_, f32[32,128]{1,0:T(8,128)S(1)} %get-tuple-element.16.refs_4_, ...), custom_call_target="tpu_custom_call" | custom-call | flops 4000000 | bytes 4000000 | tf_op jit(solution)/shard_map/inverse/pallas_call | solution.py:296
  31.0 0.0 collective-permute-done.10.refs_2_
  31.0 0.0 collective-permute-done.11.refs_3_
  31.0 0.0 collective-permute-done.9.refs_1_
  31.0 0.5 %solve.1 = (f32[64,16]{1,0:T(8,128)S(1)}, f32[1024,128]{1,0:T(8,128)S(1)}, f32[64,256]{1,0:T(8,128)S(1)}) custom-call(f32[16,64,2048]{2,1,0:T(8,128)S(1)} %get-tuple-element.12.q_ref, f32[64,64]{1,0:T(8,128)S(1)} %inverse.1.inv_ref, f32[8,128]{1,0:T(8,128)S(1)} %add_tail.1.refs_0_, f32[8,128]{1,0:T(8,128)S(1)} %collective-permute-done.9.refs_1_, ...), custom_call_target="tpu_custom_call" | custom-call | flops 524288 | bytes 1048576 | tf_op jit(solution)/shard_map/solve/pallas_call | solution.py:398
  31.5 0.3 weigh.6
  31.9 1.6 %collective-permute-start.12 = (f32[64,512]{1,0:T(8,128)S(1)}, f32[64,512]{1,0:T(8,128)S(1)}, u32[]{:S(2)}, u32[]{:S(2)}) collective-permute-start(f32[64,512]{1,0:T(8,128)S(1)} %weigh.6), channel_id=1, source_target_pairs={{0,16},{16,0},{1,17},{17,1},{2,18},{18,2},{3,19},{19,3},{4,20},{20... | collective-permute-start | bytes 393224 | tf_op jit(solution)/shard_map/ppermute | solution.py:464
  33.4 0.5 %collective-permute-start.16 = (f32[64,256]{1,0:T(8,128)S(1)}, f32[64,256]{1,0:T(8,128)S(1)}, u32[]{:S(2)}, u32[]{:S(2)}) collective-permute-start(f32[64,256]{1,0:T(8,128)S(1)} %get-tuple-element.21), channel_id=1, source_target_pairs={{0,16},{16,0},{1,17},{17,1},{2,18},{18,2},{3,19},{19,3},{4,20},{20... | collective-permute-start | bytes 196616 | tf_op jit(solution)/shard_map/ppermute | solution.py:464
  34.0 0.2 weigh.8
  34.1 1.6 %collective-permute-start.14 = (f32[64,256]{1,0:T(8,128)S(1)}, f32[64,256]{1,0:T(8,128)S(1)}, u32[]{:S(2)}, u32[]{:S(2)}) collective-permute-start(f32[64,256]{1,0:T(8,128)S(1)} %weigh.8), channel_id=1, source_target_pairs={{0,16},{16,0},{1,17},{17,1},{2,18},{18,2},{3,19},{19,3},{4,20},{20... | collective-permute-start | bytes 196616 | tf_op jit(solution)/shard_map/ppermute | solution.py:464
  35.7 0.2 weigh.9.kept_ref
  35.9 0.2 weigh.7.kept_ref
  36.0 0.3 weigh.5.kept_ref
  36.4 2.9 %collective-permute-done.16.got_ref = f32[64,256]{1,0:T(8,128)S(1)} collective-permute-done((f32[64,256]{1,0:T(8,128)S(1)}, f32[64,256]{1,0:T(8,128)S(1)}, u32[]{:S(2)}, u32[]{:S(2)}) %collective-permute-start.16) | collective-permute-done | bytes 65568 | tf_op jit(solution)/shard_map/ppermute | solution.py:464
  39.2 2.0 %collective-permute-start.17 = (f32[64,256]{1,0:T(8,128)S(1)}, f32[64,256]{1,0:T(8,128)S(1)}, u32[]{:S(2)}, u32[]{:S(2)}) collective-permute-start(f32[64,256]{1,0:T(8,128)S(1)} %split_sums.5), channel_id=1, source_target_pairs={{0,3},{1,2},{2,1},{3,0},{4,7},{5,6},{6,5},{7,4},{8,11},{9,10},{10,... | collective-permute-start | bytes 196616 | tf_op jit(solution)/shard_map/ppermute | solution.py:464
  41.2 0.0 collective-permute-done.14.got_ref
  41.2 0.2 collective-permute-start.15
  41.4 0.0 collective-permute-done.12.got_ref
  41.5 2.4 %collective-permute-start.13 = (f32[64,256]{1,0:T(8,128)S(1)}, f32[64,256]{1,0:T(8,128)S(1)}, u32[]{:S(2)}, u32[]{:S(2)}) collective-permute-start(f32[64,256]{1,0:T(8,128)S(1)} %get-tuple-element.20), channel_id=1, source_target_pairs={{0,1},{1,0},{2,3},{3,2},{4,5},{5,4},{6,7},{7,6},{8,9},{9,8},{10,11... | collective-permute-start | bytes 196616 | tf_op jit(solution)/shard_map/ppermute | solution.py:464
  43.9 0.7 %own_row.1 = f32[1,64]{1,0:T(1,128)} custom-call(f32[64,16]{1,0:T(8,128)S(1)} %get-tuple-element.17.factors_ref), custom_call_target="tpu_custom_call" | custom-call | tf_op jit(solution)/shard_map/own_row/pallas_call | solution.py:369
  44.6 1.3 %collective-permute-done.17.refs_3_ = f32[64,256]{1,0:T(8,128)S(1)} collective-permute-done((f32[64,256]{1,0:T(8,128)S(1)}, f32[64,256]{1,0:T(8,128)S(1)}, u32[]{:S(2)}, u32[]{:S(2)}) %collective-permute-start.17) | collective-permute-done | bytes 65568 | tf_op jit(solution)/shard_map/ppermute | solution.py:464
  45.9 1.3 %collective-permute-done.15.refs_2_ = f32[64,256]{1,0:T(8,128)S(1)} collective-permute-done((f32[64,256]{1,0:T(8,128)S(1)}, f32[64,256]{1,0:T(8,128)S(1)}, u32[]{:S(2)}, u32[]{:S(2)}) %collective-permute-start.15) | collective-permute-done | bytes 65568 | tf_op jit(solution)/shard_map/ppermute | solution.py:464
  47.2 0.0 collective-permute-done.13.refs_1_
  47.2 0.7 %final_sum.1 = f32[64,1,256]{2,1,0:T(1,128)} custom-call(f32[64,256]{1,0:T(8,128)S(1)} %get-tuple-element.19.refs_0_, f32[64,256]{1,0:T(8,128)S(1)} %collective-permute-done.13.refs_1_, f32[64,256]{1,0:T(8,128)S(1)} %collective-permute-done.15.refs_2_, f32[64,256]{1,0:T(8,128)S(1)} %collective-permute-done.17.refs_3_), custom_call_target="tpu_custom_call" | custom-call | tf_op jit(solution)/shard_map/final_sum/pallas_call | solution.py:452
  (6 shorter events, 0.0 us)
Async XLA Ops:
  0.6 16.2 %copy-start = (f32[512,64]{0,1:T(8,128)S(1)}, f32[512,64]{0,1:T(8,128)}, u32[]{:S(2)}) copy-start(f32[512,64]{0,1:T(8,128)} %param.4) | copy-start | bytes 393220
  0.6 10.8 %collective-permute-start = (f32[64,512]{1,0:T(8,128)}, f32[64,512]{1,0:T(8,128)S(1)}, u32[]{:S(2)}, u32[]{:S(2)}) collective-permute-start(f32[64,512]{1,0:T(8,128)} %bitcast.1), channel_id=1, source_target_pairs={{0,1},{1,0},{2,3},{3,2},{4,5},{5,4},{6,7},{7,6},{8,9},{9,8},{10,11... | collective-permute-start | bytes 393224 | tf_op jit(solution)/shard_map/ppermute | solution.py:464
  3.8 13.1 %collective-permute-start.1 = (f32[64,512]{1,0:T(8,128)}, f32[64,512]{1,0:T(8,128)S(1)}, u32[]{:S(2)}, u32[]{:S(2)}) collective-permute-start(f32[64,512]{1,0:T(8,128)} %bitcast.2), channel_id=1, source_target_pairs={{0,2},{1,3},{2,0},{3,1},{4,6},{5,7},{6,4},{7,5},{8,10},{9,11},{10,... | collective-permute-start | bytes 393224 | tf_op jit(solution)/shard_map/ppermute | solution.py:464
  6.3 11.7 %collective-permute-start.2 = (f32[64,512]{1,0:T(8,128)}, f32[64,512]{1,0:T(8,128)S(1)}, u32[]{:S(2)}, u32[]{:S(2)}) collective-permute-start(f32[64,512]{1,0:T(8,128)} %bitcast.3), channel_id=1, source_target_pairs={{0,3},{1,2},{2,1},{3,0},{4,7},{5,6},{6,5},{7,4},{8,11},{9,10},{10,... | collective-permute-start | bytes 393224 | tf_op jit(solution)/shard_map/ppermute | solution.py:464
  18.6 4.8 %collective-permute-start.3 = (f32[40,128]{1,0:T(8,128)S(1)}, f32[40,128]{1,0:T(8,128)S(1)}, u32[]{:S(2)}, u32[]{:S(2)}) collective-permute-start(f32[40,128]{1,0:T(8,128)S(1)} %mode_one_late.1.refs_0_), channel_id=1, source_target_pairs={{0,4},{4,0},{8,12},{12,8},{1,5},{5,1},{9,13},{13,9},{2,6},{6,2},{1... | collective-permute-start | bytes 61448 | tf_op jit(solution)/shard_map/ppermute | solution.py:464
  18.7 6.2 %collective-permute-start.4 = (f32[40,128]{1,0:T(8,128)S(1)}, f32[40,128]{1,0:T(8,128)S(1)}, u32[]{:S(2)}, u32[]{:S(2)}) collective-permute-start(f32[40,128]{1,0:T(8,128)S(1)} %mode_one_late.1.refs_0_), channel_id=1, source_target_pairs={{0,8},{4,12},{8,0},{12,4},{1,9},{5,13},{9,1},{13,5},{2,10},{6,14},... | collective-permute-start | bytes 61448 | tf_op jit(solution)/shard_map/ppermute | solution.py:464
  20.2 4.7 %collective-permute-start.5 = (f32[40,128]{1,0:T(8,128)S(1)}, f32[40,128]{1,0:T(8,128)S(1)}, u32[]{:S(2)}, u32[]{:S(2)}) collective-permute-start(f32[40,128]{1,0:T(8,128)S(1)} %mode_one_late.1.refs_0_), channel_id=1, source_target_pairs={{0,12},{4,8},{8,4},{12,0},{1,13},{5,9},{9,5},{13,1},{2,14},{6,10},... | collective-permute-start | bytes 61448 | tf_op jit(solution)/shard_map/ppermute | solution.py:464
  20.5 6.5 %collective-permute-start.6 = (f32[32,128]{1,0:T(8,128)S(1)}, f32[32,128]{1,0:T(8,128)S(1)}, u32[]{:S(2)}, u32[]{:S(2)}) collective-permute-start(f32[32,128]{1,0:T(8,128)S(1)} %get-tuple-element.16.refs_4_), channel_id=1, source_target_pairs={{0,1},{1,0},{2,3},{3,2},{4,5},{5,4},{6,7},{7,6},{8,9},{9,8},{10,11... | collective-permute-start | bytes 49160 | tf_op jit(solution)/shard_map/ppermute | solution.py:464
  21.3 6.2 %collective-permute-start.7 = (f32[32,128]{1,0:T(8,128)S(1)}, f32[32,128]{1,0:T(8,128)S(1)}, u32[]{:S(2)}, u32[]{:S(2)}) collective-permute-start(f32[32,128]{1,0:T(8,128)S(1)} %get-tuple-element.16.refs_4_), channel_id=1, source_target_pairs={{0,2},{1,3},{2,0},{3,1},{4,6},{5,7},{6,4},{7,5},{8,10},{9,11},{10,... | collective-permute-start | bytes 49160 | tf_op jit(solution)/shard_map/ppermute | solution.py:464
  23.3 5.5 %collective-permute-start.8 = (f32[32,128]{1,0:T(8,128)S(1)}, f32[32,128]{1,0:T(8,128)S(1)}, u32[]{:S(2)}, u32[]{:S(2)}) collective-permute-start(f32[32,128]{1,0:T(8,128)S(1)} %get-tuple-element.16.refs_4_), channel_id=1, source_target_pairs={{0,3},{1,2},{2,1},{3,0},{4,7},{5,6},{6,5},{7,4},{8,11},{9,10},{10,... | collective-permute-start | bytes 49160 | tf_op jit(solution)/shard_map/ppermute | solution.py:464
  24.9 6.1 %collective-permute-start.10 = (f32[8,128]{1,0:T(8,128)S(1)}, f32[8,128]{1,0:T(8,128)S(1)}, u32[]{:S(2)}, u32[]{:S(2)}) collective-permute-start(f32[8,128]{1,0:T(8,128)S(1)} %add_tail.1.refs_0_), channel_id=1, source_target_pairs={{0,6},{1,7},{2,4},{3,5},{4,2},{5,3},{6,0},{7,1},{8,14},{9,15},{10,... | collective-permute-start | bytes 12296 | tf_op jit(solution)/shard_map/ppermute | solution.py:477
  25.0 6.0 %collective-permute-start.11 = (f32[8,128]{1,0:T(8,128)S(1)}, f32[8,128]{1,0:T(8,128)S(1)}, u32[]{:S(2)}, u32[]{:S(2)}) collective-permute-start(f32[8,128]{1,0:T(8,128)S(1)} %add_tail.1.refs_0_), channel_id=1, source_target_pairs={{0,7},{1,6},{2,5},{3,4},{4,3},{5,2},{6,1},{7,0},{8,15},{9,14},{10,... | collective-permute-start | bytes 12296 | tf_op jit(solution)/shard_map/ppermute | solution.py:477
  27.0 4.1 %collective-permute-start.9 = (f32[8,128]{1,0:T(8,128)S(1)}, f32[8,128]{1,0:T(8,128)S(1)}, u32[]{:S(2)}, u32[]{:S(2)}) collective-permute-start(f32[8,128]{1,0:T(8,128)S(1)} %add_tail.1.refs_0_), channel_id=1, source_target_pairs={{0,5},{1,4},{2,7},{3,6},{4,1},{5,0},{6,3},{7,2},{8,13},{9,12},{10,... | collective-permute-start | bytes 12296 | tf_op jit(solution)/shard_map/ppermute | solution.py:477
  31.9 9.6 %collective-permute-start.12 = (f32[64,512]{1,0:T(8,128)S(1)}, f32[64,512]{1,0:T(8,128)S(1)}, u32[]{:S(2)}, u32[]{:S(2)}) collective-permute-start(f32[64,512]{1,0:T(8,128)S(1)} %weigh.6), channel_id=1, source_target_pairs={{0,16},{16,0},{1,17},{17,1},{2,18},{18,2},{3,19},{19,3},{4,20},{20... | collective-permute-start | bytes 393224 | tf_op jit(solution)/shard_map/ppermute | solution.py:464
  33.4 5.8 %collective-permute-start.16 = (f32[64,256]{1,0:T(8,128)S(1)}, f32[64,256]{1,0:T(8,128)S(1)}, u32[]{:S(2)}, u32[]{:S(2)}) collective-permute-start(f32[64,256]{1,0:T(8,128)S(1)} %get-tuple-element.21), channel_id=1, source_target_pairs={{0,16},{16,0},{1,17},{17,1},{2,18},{18,2},{3,19},{19,3},{4,20},{20... | collective-permute-start | bytes 196616 | tf_op jit(solution)/shard_map/ppermute | solution.py:464
  34.1 7.1 %collective-permute-start.14 = (f32[64,256]{1,0:T(8,128)S(1)}, f32[64,256]{1,0:T(8,128)S(1)}, u32[]{:S(2)}, u32[]{:S(2)}) collective-permute-start(f32[64,256]{1,0:T(8,128)S(1)} %weigh.8), channel_id=1, source_target_pairs={{0,16},{16,0},{1,17},{17,1},{2,18},{18,2},{3,19},{19,3},{4,20},{20... | collective-permute-start | bytes 196616 | tf_op jit(solution)/shard_map/ppermute | solution.py:464
  39.2 6.6 %collective-permute-start.17 = (f32[64,256]{1,0:T(8,128)S(1)}, f32[64,256]{1,0:T(8,128)S(1)}, u32[]{:S(2)}, u32[]{:S(2)}) collective-permute-start(f32[64,256]{1,0:T(8,128)S(1)} %split_sums.5), channel_id=1, source_target_pairs={{0,3},{1,2},{2,1},{3,0},{4,7},{5,6},{6,5},{7,4},{8,11},{9,10},{10,... | collective-permute-start | bytes 196616 | tf_op jit(solution)/shard_map/ppermute | solution.py:464
  41.2 6.0 %collective-permute-start.15 = (f32[64,256]{1,0:T(8,128)S(1)}, f32[64,256]{1,0:T(8,128)S(1)}, u32[]{:S(2)}, u32[]{:S(2)}) collective-permute-start(f32[64,256]{1,0:T(8,128)S(1)} %split_sums.4), channel_id=1, source_target_pairs={{0,2},{1,3},{2,0},{3,1},{4,6},{5,7},{6,4},{7,5},{8,10},{9,11},{10,... | collective-permute-start | bytes 196616 | tf_op jit(solution)/shard_map/ppermute | solution.py:464
  41.5 5.7 %collective-permute-start.13 = (f32[64,256]{1,0:T(8,128)S(1)}, f32[64,256]{1,0:T(8,128)S(1)}, u32[]{:S(2)}, u32[]{:S(2)}) collective-permute-start(f32[64,256]{1,0:T(8,128)S(1)} %get-tuple-element.20), channel_id=1, source_target_pairs={{0,1},{1,0},{2,3},{3,2},{4,5},{5,4},{6,7},{7,6},{8,9},{9,8},{10,11... | collective-permute-start | bytes 196616 | tf_op jit(solution)/shard_map/ppermute | solution.py:464
